TPU v7x, 512 devices: a whole 4x4x16 slice. The times are simulated.
512 devices in a mesh: node: 16 (over z), grp: 8 (over y, core), rep: 4 (over x).
Axes of the slice: x: 4, y: 4, z: 16, core: 2. Of those that a mesh axis runs over, the one named last changes fastest.
Arguments:
- tokens: bfloat16 [16384, 768], P(('node', 'grp'), 'rep'), may hold values from -6 to 6
- gates: float32 [16384, 2], P(('node', 'grp')), may hold values from 0.05 to 1
- expert_ids: int32 [16384, 2], P(('node', 'grp')), may hold values from 0 to 127, all different within a row; in each aligned block of 128 rows (0 to 127, 128 to 255, ...) at most 4 rows name the same one
- w_in: bfloat16 [128, 768, 1536], P(('node', 'grp'), None, 'rep'), may hold values from -0.21875 to 0.21875
- b_in: float32 [128, 1536], P(('node', 'grp'), 'rep'), may hold values from -3 to 3
- w_out: bfloat16 [128, 1536, 768], P(('node', 'grp'), 'rep'), may hold values from -0.15625 to 0.15625
- b_out: float32 [128, 768], P(('node', 'grp'), 'rep'), may hold values from -3 to 3
- cotangent: bfloat16 [16384, 768], P(('node', 'grp'), 'rep'), may hold values from -6 to 6
Outputs:
- mixed: bfloat16 [16384, 768], P(('node', 'grp'), 'rep')
- d_tokens: bfloat16 [16384, 768], P(('node', 'grp'), 'rep')
- d_gates: float32 [16384, 2], P(('node', 'grp'))
- d_w_in: float32 [128, 768, 1536], P(('node', 'grp'), None, 'rep')
- d_b_in: float32 [128, 1536], P(('node', 'grp'), 'rep')
- d_w_out: float32 [128, 1536, 768], P(('node', 'grp'), 'rep')
- d_b_out: float32 [128, 768], P(('node', 'grp'), 'rep')
Inputs may be any that keep to these rules, and one draw needn't show every extreme that they name: `expert_ids`: each row names 2 different experts. Among the 128 rows of one device's aligned block no expert is named more than 4 times, and in some blocks one expert is named exactly 4 times.
All inputs are finite; a program needn't handle non-finite values.
Results may differ from a plain program's by a relative error of at most 0.0064.
Values may be sent and summed in bfloat16 or wider, within the bound.
A program may use at most 64 MiB of HBM per device.

v0:
```python
import jax
import jax.numpy as jnp
from jax import lax
from jax.sharding import PartitionSpec as P


def cut_along(array, dim, length):
    dims = array.shape
    blocks = array.reshape(*dims[:dim], length, dims[dim] // length, *dims[dim + 1 :])
    return jnp.moveaxis(blocks, dim, 0)


def summed_on_arrival(array, axis, dim):
    blocks = cut_along(array, dim, lax.axis_size(axis))
    arrived = lax.all_to_all(blocks, axis, split_axis=0, concat_axis=0, tiled=True)
    return arrived.sum(axis=0)


def contract_first(left, right):
    return lax.dot_general(
        left, right, (((0,), (0,)), ((), ())), preferred_element_type=jnp.float32
    )


def contract_last(left, right):
    return lax.dot_general(
        left, right, (((1,), (1,)), ((), ())), preferred_element_type=jnp.float32
    )


def relocate(buffer):
    return lax.all_to_all(buffer, ("node", "grp"), split_axis=0, concat_axis=0, tiled=True)


def per_device(tokens, gates, expert_ids, w_in, b_in, w_out, b_out, cotangent):
    n_experts = lax.axis_size(("node", "grp"))
    tok_rows, feat_width = tokens.shape
    top_k = expert_ids.shape[1]
    assigned = tok_rows * top_k
    capacity = max(2, 2 * assigned // n_experts)
    rows_total = n_experts * capacity
    flat_ids = expert_ids.reshape(assigned)
    position = jnp.arange(assigned, dtype=jnp.int32)
    matches = (flat_ids[:, None] == flat_ids[None, :]) & (position[None, :] < position[:, None])
    slot_rank = jnp.sum(matches.astype(jnp.int32), axis=1)
    target = flat_ids * capacity + slot_rank
    placing = (jnp.arange(rows_total, dtype=jnp.int32)[:, None] == target[None, :]).astype(
        jnp.bfloat16
    )
    token_copies = jnp.repeat(tokens, top_k, axis=0)
    outbound = jnp.dot(placing, token_copies, preferred_element_type=jnp.float32).astype(
        jnp.bfloat16
    )
    inbound = relocate(outbound.reshape(n_experts, capacity, feat_width))
    expert_x = inbound.reshape(rows_total, feat_width)
    w_first = w_in[0]
    bias_first = b_in[0]
    w_second = w_out[0]
    bias_second = b_out[0]
    feat_local = w_second.shape[1] // lax.axis_size("rep")
    pre_act = jnp.dot(
        lax.all_gather(expert_x, "rep", axis=1, tiled=True),
        w_first,
        preferred_element_type=jnp.float32,
    )
    pre_act = pre_act + bias_first
    hidden = jax.nn.gelu(pre_act).astype(jnp.bfloat16)
    partial_out = jnp.dot(hidden, w_second, preferred_element_type=jnp.float32)
    summed = summed_on_arrival(partial_out, "rep", 1)
    expert_out = (summed + bias_second).astype(jnp.bfloat16)
    returned = relocate(expert_out.reshape(n_experts, capacity, feat_local)).reshape(
        rows_total, feat_local
    )
    per_assign = contract_first(placing, returned).reshape(tok_rows, top_k, feat_local)
    mixed = jnp.sum(gates[:, :, None] * per_assign, axis=1).astype(jnp.bfloat16)
    cot_wide = cotangent.astype(jnp.float32)
    gate_terms = jnp.sum(cot_wide[:, None, :] * per_assign, axis=2)
    d_gates = lax.psum(gate_terms, "rep")
    d_out = (
        (gates[:, :, None] * cot_wide[:, None, :])
        .astype(jnp.bfloat16)
        .reshape(assigned, feat_width)
    )
    grad_outbound = jnp.dot(placing, d_out, preferred_element_type=jnp.float32).astype(jnp.bfloat16)
    expert_grad = relocate(grad_outbound.reshape(n_experts, capacity, feat_width)).reshape(
        rows_total, feat_width
    )
    grad_bias_out = jnp.sum(expert_grad.astype(jnp.float32), axis=0)
    full_grad = lax.all_gather(expert_grad, "rep", axis=1, tiled=True)
    grad_w_out = contract_first(hidden, full_grad)
    d_hidden = contract_last(full_grad, w_second)
    _, pull_back = jax.vjp(jax.nn.gelu, pre_act)
    d_pre = pull_back(d_hidden)[0].astype(jnp.bfloat16)
    grad_bias_in = jnp.sum(d_pre.astype(jnp.float32), axis=0)
    grad_w_in = contract_first(lax.all_gather(expert_x, "rep", axis=1, tiled=True), d_pre)
    partial_in = contract_last(d_pre, w_first)
    row_sums = summed_on_arrival(partial_in, "rep", 1)
    d_rows = row_sums.astype(jnp.bfloat16)
    back_rows = relocate(d_rows.reshape(n_experts, capacity, feat_local)).reshape(
        rows_total, feat_local
    )
    row_grads = contract_first(placing, back_rows).reshape(tok_rows, top_k, feat_local)
    d_tokens = jnp.sum(row_grads, axis=1).astype(jnp.bfloat16)
    return (
        mixed,
        d_tokens,
        d_gates,
        grad_w_in[None],
        grad_bias_in[None],
        grad_w_out[None],
        grad_bias_out[None],
    )


def solution(mesh):
    return jax.shard_map(
        per_device,
        mesh=mesh,
        in_specs=(
            P(("node", "grp"), "rep"),
            P(("node", "grp"), None),
            P(("node", "grp"), None),
            P(("node", "grp"), None, "rep"),
            P(("node", "grp"), "rep"),
            P(("node", "grp"), "rep", None),
            P(("node", "grp"), "rep"),
            P(("node", "grp"), "rep"),
        ),
        out_specs=(
            P(("node", "grp"), "rep"),
            P(("node", "grp"), "rep"),
            P(("node", "grp"), None),
            P(("node", "grp"), None, "rep"),
            P(("node", "grp"), "rep"),
            P(("node", "grp"), "rep", None),
            P(("node", "grp"), "rep"),
        ),
        check_vma=False,
    )
```

profile of v0, /device:TPU:1, one launch (start us, length us, event | category | flops | bytes accessed | tf_op | source)
XLA Modules:
  0.0 195.7 jit_solution(1429122278033340513)
XLA Ops:
  0.7 1.0 copy.44
  1.8 0.8 copy.43
  2.8 0.2 convert_reduce_fusion.2
  3.0 0.3 convolution_convert_fusion.1
  3.4 0.8 reshape.110
  4.2 20.7 %all-to-all-start = ((bf16[128,4,192]{2,1,0:T(4,128)(2,1)}), bf16[128,4,192]{2,1,0:T(4,128)(2,1)S(1)}, u32[]{:S(2)}, u32[]{:S(2)}) async-start(bf16[128,4,192]{2,1,0:T(4,128)(2,1)} %reshape.110), calls=%async_computation | async-start | bytes 524288 | tf_op jit(solution)/shard_map/all_to_all | solution.py:32
  25.4 0.2 mul.100
  25.6 0.3 convolution_convert_fusion
  26.0 0.8 reshape.113
  26.8 0.3 copy.47
  27.2 18.2 %all-to-all-done = bf16[128,4,192]{2,1,0:T(4,128)(2,1)S(1)} async-done(((bf16[128,4,192]{2,1,0:T(4,128)(2,1)}), bf16[128,4,192]{2,1,0:T(4,128)(2,1)S(1)}, u32[]{:S(2)}, u32[]{:S(2)}) %all-to-all-start) | async-done | bytes 196640 | tf_op jit(solution)/shard_map/all_to_all | solution.py:32
  45.3 8.3 %all-to-all-start.3 = ((bf16[128,4,192]{2,1,0:T(4,128)(2,1)}), bf16[128,4,192]{2,1,0:T(4,128)(2,1)S(1)}, u32[]{:S(2)}, u32[]{:S(2)}) async-start(bf16[128,4,192]{2,1,0:T(4,128)(2,1)} %reshape.113), calls=%async_computation.3 | async-start | bytes 524288 | tf_op jit(solution)/shard_map/all_to_all | solution.py:32
  53.6 0.2 reshape.111
  53.9 12.6 %all_gather.7 = bf16[512,768]{0,1:T(8,128)(2,1)S(1)} all-gather(bf16[512,192]{0,1:T(8,128)(2,1)S(1)} %copy.46), channel_id=1, replica_groups=mesh['node'=16,'grp'=8,'rep'=4] {'rep'}, dimensions={1}, use_global_device_ids=true | all-gather | bytes 983040 | tf_op jit(solution)/shard_map/all_gather | solution.py:62
  66.5 0.6 convolution_add_fusion
  67.2 0.9 copy-done.3
  68.0 1.9 convolution_bitcast_fusion.1
  69.9 4.2 %all-to-all-done.3 = bf16[128,4,192]{2,1,0:T(4,128)(2,1)S(1)} async-done(((bf16[128,4,192]{2,1,0:T(4,128)(2,1)}), bf16[128,4,192]{2,1,0:T(4,128)(2,1)S(1)}, u32[]{:S(2)}, u32[]{:S(2)}) %all-to-all-start.3) | async-done | bytes 196640 | tf_op jit(solution)/shard_map/all_to_all | solution.py:32
  74.1 4.0 %all-to-all-start.1 = ((f32[4,512,192]{1,2,0:T(8,128)}), f32[4,512,192]{1,2,0:T(8,128)S(1)}, u32[]{:S(2)}, u32[]{:S(2)}) async-start(f32[4,512,192]{1,2,0:T(8,128)} %convolution_bitcast_fusion.1), calls=%async_computation.1 | async-start | bytes 3145728 | tf_op jit(solution)/shard_map/all_to_all | solution.py:15
  78.1 0.2 reshape.114
  78.3 0.8 copy.54
  79.1 25.8 %all_gather.8 = bf16[512,768]{0,1:T(8,128)(2,1)S(1)} all-gather(bf16[512,192]{0,1:T(8,128)(2,1)} %copy.54), channel_id=1, replica_groups=mesh['node'=16,'grp'=8,'rep'=4] {'rep'}, dimensions={1}, use_global_device_ids=true | all-gather | bytes 983040 | tf_op jit(solution)/shard_map/all_gather | solution.py:89
  104.9 2.6 %convert_reduce_fusion = (f32[384]{0:T(512)S(1)}, bf16[512,384]{1,0:T(8,128)(2,1)S(1)}) fusion(f32[512,384]{1,0:T(8,128)} %copy-done.3, bf16[512,768]{0,1:T(8,128)(2,1)S(1)} %all_gather.8, bf16[1,384,768]{2,1,0:T(8,128)(2,1)} %param.13), kind=kOutput, calls=%fused_computation.17 | convolution fusion | flops 306314880 | bytes 2557440 | tf_op jit(solution)/shard_map/dot_general | solution.py:26
  107.5 0.7 copy-done.1
  108.2 1.7 convolution_bitcast_fusion
  110.0 4.3 %all-to-all-start.4 = ((f32[4,512,192]{1,2,0:T(8,128)}), f32[4,512,192]{1,2,0:T(8,128)}, u32[]{:S(2)}, u32[]{:S(2)}) async-start(f32[4,512,192]{1,2,0:T(8,128)} %convolution_bitcast_fusion), calls=%async_computation.4 | async-start | bytes 3145728 | tf_op jit(solution)/shard_map/all_to_all | solution.py:15
  114.3 0.9 reduce_sum.75
  115.3 1.2 copy.48
  116.5 0.2 reduce_sum.76
  116.6 0.8 add_convert_fusion
  117.4 13.0 %all-to-all-done.4 = f32[4,512,192]{1,2,0:T(8,128)} async-done(((f32[4,512,192]{1,2,0:T(8,128)}), f32[4,512,192]{1,2,0:T(8,128)}, u32[]{:S(2)}, u32[]{:S(2)}) %all-to-all-start.4) | async-done | bytes 1572896 | tf_op jit(solution)/shard_map/all_to_all | solution.py:15
  130.4 15.1 %all-to-all-start.2 = ((bf16[128,4,192]{2,1,0:T(4,128)(2,1)}), bf16[128,4,192]{2,1,0:T(4,128)(2,1)S(1)}, u32[]{:S(2)}, u32[]{:S(2)}) async-start(bf16[128,4,192]{2,1,0:T(4,128)(2,1)} %add_convert_fusion), calls=%async_computation.2 | async-start | bytes 524288 | tf_op jit(solution)/shard_map/all_to_all | solution.py:32
  145.5 1.6 reduce_sum.78
  147.2 0.8 convert_element_type.57
  148.0 17.9 %all-to-all-done.2 = bf16[128,4,192]{2,1,0:T(4,128)(2,1)S(1)} async-done(((bf16[128,4,192]{2,1,0:T(4,128)(2,1)}), bf16[128,4,192]{2,1,0:T(4,128)(2,1)S(1)}, u32[]{:S(2)}, u32[]{:S(2)}) %all-to-all-start.2) | async-done | bytes 196640 | tf_op jit(solution)/shard_map/all_to_all | solution.py:32
  165.9 8.3 %all-to-all-start.5 = ((bf16[128,4,192]{2,1,0:T(4,128)(2,1)}), bf16[128,4,192]{2,1,0:T(4,128)(2,1)S(1)}, u32[]{:S(2)}, u32[]{:S(2)}) async-start(bf16[128,4,192]{2,1,0:T(4,128)(2,1)} %convert_element_type.57), calls=%async_computation.5 | async-start | bytes 524288 | tf_op jit(solution)/shard_map/all_to_all | solution.py:32
  174.4 0.6 convert_element_type.52
  175.1 0.9 eq.50
  175.9 0.6 broadcast_in_dim.12
  176.5 0.7 convert_reduce_fusion.1
  177.2 1.6 convolution_bitcast_fusion.3
  178.8 1.7 convolution_bitcast_fusion.2
  180.5 0.2 reshape.112
  180.7 0.9 multiply_reduce_fusion
  181.6 8.0 %psum.7 = f32[128,2]{0,1:T(2,128)} all-reduce(f32[128,2]{0,1:T(2,128)S(1)} %get-tuple-element.7), channel_id=1, replica_groups=mesh['node'=16,'grp'=8,'rep'=4] {'rep'}, use_global_device_ids=true, to_apply=%region_6.0 | all-reduce | flops 256 | bytes 2048 | tf_op jit(solution)/shard_map/psum | solution.py:78
  189.6 5.1 %all-to-all-done.5 = bf16[128,4,192]{2,1,0:T(4,128)(2,1)S(1)} async-done(((bf16[128,4,192]{2,1,0:T(4,128)(2,1)}), bf16[128,4,192]{2,1,0:T(4,128)(2,1)S(1)}, u32[]{:S(2)}, u32[]{:S(2)}) %all-to-all-start.5) | async-done | bytes 196640 | tf_op jit(solution)/shard_map/all_to_all | solution.py:32
  194.7 0.2 reshape.115
  194.9 0.9 convolution_reduce_fusion
  (41 shorter events, 1.5 us)
Async XLA Ops:
  0.6 65.9 %copy-start = (bf16[1,768,384]{2,1,0:T(8,128)(2,1)S(1)}, bf16[1,768,384]{2,1,0:T(8,128)(2,1)}, u32[]{:S(2)}) copy-start(bf16[1,768,384]{2,1,0:T(8,128)(2,1)} %param.11) | copy-start | bytes 1769476
  0.6 24.2 %copy-start.13 = (f32[128,2]{0,1:T(2,128)S(1)}, f32[128,2]{0,1:T(2,128)}, u32[]{:S(2)}) copy-start(f32[128,2]{0,1:T(2,128)} %param.9) | copy-start | bytes 3076
  0.7 24.5 %copy-start.9 = (bf16[128,192]{0,1:T(8,128)(2,1)S(1)}, bf16[128,192]{0,1:T(8,128)(2,1)}, u32[]{:S(2)}) copy-start(bf16[128,192]{0,1:T(8,128)(2,1)} %param.15) | copy-start | bytes 147460
  4.2 22.6 %copy-start.7 = (bf16[1,384,768]{2,1,0:T(8,128)(2,1)S(1)}, bf16[1,384,768]{2,1,0:T(8,128)(2,1)}, u32[]{:S(2)}) copy-start(bf16[1,384,768]{2,1,0:T(8,128)(2,1)} %param.13) | copy-start | bytes 1769476
  4.2 41.1 %all-to-all-start = ((bf16[128,4,192]{2,1,0:T(4,128)(2,1)}), bf16[128,4,192]{2,1,0:T(4,128)(2,1)S(1)}, u32[]{:S(2)}, u32[]{:S(2)}) async-start(bf16[128,4,192]{2,1,0:T(4,128)(2,1)} %reshape.110), calls=%async_computation | async-start | bytes 524288 | tf_op jit(solution)/shard_map/all_to_all | solution.py:32
  25.4 1.8 copy-start.11
  45.3 28.8 %all-to-all-start.3 = ((bf16[128,4,192]{2,1,0:T(4,128)(2,1)}), bf16[128,4,192]{2,1,0:T(4,128)(2,1)S(1)}, u32[]{:S(2)}, u32[]{:S(2)}) async-start(bf16[128,4,192]{2,1,0:T(4,128)(2,1)} %reshape.113), calls=%async_computation.3 | async-start | bytes 524288 | tf_op jit(solution)/shard_map/all_to_all | solution.py:32
  67.1 0.9 copy-start.3
  74.1 35.9 %all-to-all-start.1 = ((f32[4,512,192]{1,2,0:T(8,128)}), f32[4,512,192]{1,2,0:T(8,128)S(1)}, u32[]{:S(2)}, u32[]{:S(2)}) async-start(f32[4,512,192]{1,2,0:T(8,128)} %convolution_bitcast_fusion.1), calls=%async_computation.1 | async-start | bytes 3145728 | tf_op jit(solution)/shard_map/all_to_all | solution.py:15
  104.9 2.6 %copy-start.5 = (bf16[512,768]{0,1:T(8,128)(2,1)}, bf16[512,768]{0,1:T(8,128)(2,1)S(1)}, u32[]{:S(2)}) copy-start(bf16[512,768]{0,1:T(8,128)(2,1)S(1)} %all_gather.8) | copy-start | bytes 2359300
  107.5 0.7 copy-start.1
  110.0 20.4 %all-to-all-start.4 = ((f32[4,512,192]{1,2,0:T(8,128)}), f32[4,512,192]{1,2,0:T(8,128)}, u32[]{:S(2)}, u32[]{:S(2)}) async-start(f32[4,512,192]{1,2,0:T(8,128)} %convolution_bitcast_fusion), calls=%async_computation.4 | async-start | bytes 3145728 | tf_op jit(solution)/shard_map/all_to_all | solution.py:15
  114.3 2.3 %copy-start.12 = (f32[1,192]{1,0:T(1,128)S(1)}, f32[1,192]{1,0:T(1,128)}, u32[]{:S(2)}) copy-start(f32[1,192]{1,0:T(1,128)} %param.14) | copy-start | bytes 2308
  130.4 35.5 %all-to-all-start.2 = ((bf16[128,4,192]{2,1,0:T(4,128)(2,1)}), bf16[128,4,192]{2,1,0:T(4,128)(2,1)S(1)}, u32[]{:S(2)}, u32[]{:S(2)}) async-start(bf16[128,4,192]{2,1,0:T(4,128)(2,1)} %add_convert_fusion), calls=%async_computation.2 | async-start | bytes 524288 | tf_op jit(solution)/shard_map/all_to_all | solution.py:32
  147.1 30.1 %copy-start.2 = (bf16[512,384]{1,0:T(8,128)(2,1)S(1)}, bf16[512,384]{1,0:T(8,128)(2,1)}, u32[]{:S(2)}) copy-start(bf16[512,384]{1,0:T(8,128)(2,1)} %copy-done.1) | copy-start | bytes 1179652
  165.9 28.8 %all-to-all-start.5 = ((bf16[128,4,192]{2,1,0:T(4,128)(2,1)}), bf16[128,4,192]{2,1,0:T(4,128)(2,1)S(1)}, u32[]{:S(2)}, u32[]{:S(2)}) async-start(bf16[128,4,192]{2,1,0:T(4,128)(2,1)} %convert_element_type.57), calls=%async_computation.5 | async-start | bytes 524288 | tf_op jit(solution)/shard_map/all_to_all | solution.py:32
  174.4 4.4 %copy-start.4 = (f32[512,384]{1,0:T(8,128)S(1)}, f32[512,384]{1,0:T(8,128)}, u32[]{:S(2)}) copy-start(f32[512,384]{1,0:T(8,128)} %copy-done.3) | copy-start | bytes 2359300
  175.9 2.9 %copy-start.6 = (bf16[512,768]{0,1:T(8,128)(2,1)S(1)}, bf16[512,768]{0,1:T(8,128)(2,1)}, u32[]{:S(2)}) copy-start(bf16[512,768]{0,1:T(8,128)(2,1)} %copy-done.5) | copy-start | bytes 2359300
  178.8 1.9 copy-start.8
  178.8 1.9 copy-start.10
where the time goes:
time: 197 us; the launch traced here: 196 us
  starting transfers between devices  60.8 us (31%)
  waiting for transfers between devices  58.3 us (30%)
  blocking collectives  46.4 us (24%)
  matrix products  12.5 us (6%)
  local copies, waits for them, and re-layouts  11.7 us (6%)
  other arithmetic  5.04 us (3%)
    all_to_all x4, starting transfers between devices, relocate(): lax.all_to_all(buffer, ('node', 'grp'), split_axis=0, concat_axis=0, tile...  52.4 us
    all_to_all x4, waiting for transfers between devices, relocate(): lax.all_to_all(buffer, ('node', 'grp'), split_axis=0, concat_axis=0, tile...  45.4 us
    all_gather x1, blocking collectives, per_device(): full_grad = lax.all_gather(expert_grad, 'rep', axis=1, tiled=True)  25.8 us
    all_to_all x2, waiting for transfers between devices, summed_on_arrival(): lax.all_to_all(blocks, axis, split_axis=0, concat_axis=0, tiled=True)  13 us
    all_gather x1, blocking collectives, per_device(): lax.all_gather(expert_x, 'rep', axis=1, tiled=True)  12.6 us
    all_to_all x2, starting transfers between devices, summed_on_arrival(): lax.all_to_all(blocks, axis, split_axis=0, concat_axis=0, tiled=True)  8.35 us
    psum x1, blocking collectives, per_device(): d_gates = lax.psum(gate_terms, 'rep')  7.99 us
    dot_general x4, matrix products, contract_first(): lax.dot_general(left, right, (((0,), (0,)), ((), ())), preferred_element_...  5.08 us
  transfers between devices with their start and end apart: 6, of which 5 were waited for; matrix products, arithmetic and copies ran while one was open for 12% of the time, Pallas kernels for 0%

commit v1 on v0

v1 whole, which is shorter than its diff:
```python
import functools
import math

import jax
import jax.numpy as jnp
from jax import lax
from jax.experimental import pallas as pl
from jax.experimental.pallas import tpu as pltpu
from jax.sharding import PartitionSpec as P

MESH = pl.DeviceIdType.MESH
CAP = 4
BF = jnp.bfloat16
F32 = jnp.float32
ROOT = math.sqrt(2.0 / math.pi)


def dot(a, b, ca, cb):
    return lax.dot_general(a, b, (((ca,), (cb,)), ((), ())), preferred_element_type=F32)


def fused(
    N, G, R,
    tok, cot, ids, gates, w_in, b_in, w_out, b_out,
    mixed, d_tok, d_gates, d_w_in, d_b_in, d_w_out, d_b_out,
    zt, zc, zm, onehot, ysend, yrecv, xall, w_out_t, pre, dgelu, hid, d_pre,
    xhalf, xfull, rhalf, rfull, back, yret, zs, zr, gs, gr, dsum, drecv,
    z_send, z_recv, y_send, y_recv, x_send, x_recv, r_send, r_recv,
    b_send, b_recv, s_send, s_recv, p_send, p_recv,
):
    n, g, r = lax.axis_index("node"), lax.axis_index("grp"), lax.axis_index("rep")
    F, T = tok.shape
    D, H = w_in.shape
    U = N // 2
    V = U // 2
    Q = V * 8
    S = 2 * G * Q
    HF, FB = F // 2, F - 128

    def at(axis, index):
        return {axis: index}

    right_z, left_z = lax.rem(n + 1, N), lax.rem(n + N - 1, N)
    right_x, left_x = lax.rem(r + 1, R), lax.rem(r + R - 1, R)
    far_x = lax.rem(r + 2, R)

    barrier = pltpu.get_barrier_semaphore()
    peers = [at("node", right_z), at("node", left_z)]
    peers += [at("grp", lax.rem(g + j, G)) for j in range(1, G)]
    peers += [at("rep", lax.rem(r + j, R)) for j in range(1, R)]
    for peer in peers:
        pl.semaphore_signal(barrier, inc=1, device_id=peer, device_id_type=MESH)
    pl.semaphore_wait(barrier, len(peers))

    def remote(src, dst, send, recv, peer):
        return pltpu.make_async_remote_copy(
            src_ref=src, dst_ref=dst, send_sem=send, recv_sem=recv,
            device_id=peer, device_id_type=MESH,
        )

    @functools.cache
    def z_copies(which, d):
        own, buf = ((tok, zt), (cot, zc), (None, zm))[which]
        src_r = buf.at[N - d + 1] if d > 1 else (own if which < 2 else buf.at[0])
        src_l = buf.at[d - 1] if d > 1 else (own if which < 2 else buf.at[0])
        if d < U:
            right = (src_r, buf.at[N - d])
            left = (src_l, buf.at[d])
        elif which < 2:
            right = (src_r.at[pl.ds(0, HF)], buf.at[U, pl.ds(0, HF)])
            left = (src_l.at[pl.ds(HF, HF)], buf.at[U, pl.ds(HF, HF)])
        else:
            right, left = (src_r, buf.at[U]), None
        found = [
            remote(*right, z_send.at[which, 0, d - 1], z_recv.at[which, 0, d - 1], at("node", right_z))
        ]
        if left is not None:
            found.append(
                remote(*left, z_send.at[which, 1, d - 1], z_recv.at[which, 1, d - 1], at("node", left_z))
            )
        return found

    started = []

    def start(copies):
        for copy in copies:
            copy.start()
        started.extend(copies)

    start(z_copies(0, 1) + z_copies(1, 1))

    ids_f = ids[...].astype(F32)
    rows = [ids_f[k : k + 1, :] for k in range(2)]
    cols = [jnp.broadcast_to(row, (T, T)).T for row in rows]
    earlier = lax.broadcasted_iota(jnp.int32, (T, T), 0) < lax.broadcasted_iota(jnp.int32, (T, T), 1)
    meta = []
    for k in range(2):
        same = jnp.where(cols[0] == rows[k], 1.0, 0.0) + jnp.where(cols[1] == rows[k], 1.0, 0.0)
        rank = jnp.sum(jnp.where(earlier, same, 0.0), axis=0, keepdims=True)
        meta.append(rows[k] * CAP + rank)
    zm[0] = jnp.concatenate(
        meta + [gates[0:1, :], gates[1:2, :], jnp.zeros((4, T), F32)], axis=0
    )
    start(z_copies(2, 1))

    row = lax.broadcasted_iota(jnp.int32, (G * 8, T), 0)
    inner = lax.rem(row, 8)
    code = (n * G + row // 8) * CAP + lax.rem(inner, 4)
    codes = [jnp.where(inner // 4 == p, code, -1).astype(F32) for p in range(2)]

    w_out_t[...] = w_out[...].T

    def pair(u):
        return (u + 1, N - u - 1) if u < U - 1 else (0, U)

    def select(u):
        h, v = u // V, u % V
        slots = pair(u)
        info = [zm[s] for s in slots]
        hot = []
        weight = jnp.zeros((G * 8, 1), F32)
        for k in range(2):
            parts = [jnp.where(info[p][k : k + 1, :] == codes[p], 1.0, 0.0) for p in range(2)]
            for p in range(2):
                weight += jnp.sum(parts[p] * info[p][2 + k : 3 + k, :], axis=1, keepdims=True)
            both = jnp.concatenate(parts, axis=1)
            hot.append(both)
            onehot[u, k] = both.astype(BF)
        place = (hot[0] + hot[1]).astype(BF)
        for which, buf in ((0, zt), (1, zc)):
            got = None
            for p, slot in enumerate(slots):
                block = (tok, cot)[which][...] if slot == 0 else buf[slot]
                part = dot(place[:, p * T : (p + 1) * T], block, 1, 1)
                got = part if got is None else got + part
            if which == 1:
                got = got * weight
            got = got.reshape(G, 8, F)
            ysend[which, :, h, v * 8 : v * 8 + 8, :] = got[:, :, 0:128].astype(BF)
            ysend[which, :, 2, v * 8 : v * 8 + 8, h * FB : (h + 1) * FB] = got[:, :, 128:F].astype(BF)

    for d in range(1, U + 1):
        for which in (2, 0, 1):
            for copy in z_copies(which, d):
                copy.wait_recv()
            if d < U:
                start(z_copies(which, d + 1))
        select(d - 1)

    @functools.cache
    def y_copies(which):
        return [
            remote(
                ysend.at[which, lax.rem(g + j, G)], yrecv.at[which, :, g],
                y_send.at[which, j - 1], y_recv.at[which, j - 1], at("grp", lax.rem(g + j, G)),
            )
            for j in range(1, G)
        ]

    for which in range(2):
        start(y_copies(which))
    for which in range(2):
        yrecv[which, :, g] = ysend[which, g]

    @functools.cache
    def x_near(which):
        own = xall.at[which, r]
        return [
            remote(own, own, x_send.at[which, 0], x_recv.at[which, 0], at("rep", right_x)),
            remote(own, own, x_send.at[which, 1], x_recv.at[which, 1], at("rep", left_x)),
        ]

    @functools.cache
    def x_relay(which):
        top = xall.at[which, left_x, pl.ds(0, HF)]
        low = xall.at[which, right_x, pl.ds(HF, HF)]
        return [
            remote(top, top, x_send.at[which, 2], x_recv.at[which, 2], at("rep", right_x)),
            remote(low, low, x_send.at[which, 3], x_recv.at[which, 3], at("rep", left_x)),
        ]

    def unpack(which):
        rows_of = G * Q
        for h in range(2):
            xall[which, r, 0:128, h * rows_of : (h + 1) * rows_of] = (
                yrecv[which, h].reshape(rows_of, 128).T
            )
        low = yrecv[which, 2].reshape(rows_of, 128).T
        for h in range(2):
            xall[which, r, 128:F, h * rows_of : (h + 1) * rows_of] = low[h * FB : (h + 1) * FB]

    for which in range(2):
        for copy in y_copies(which):
            copy.wait_recv()
        unpack(which)
        start(x_near(which))

    def relay(which):
        near, passed = x_near(which), x_relay(which)
        for i in range(2):
            near[i].wait_recv()
            start([passed[i]])

    def arrive(which):
        for copy in x_relay(which):
            copy.wait_recv()

    relay(0)
    arrive(0)
    x_full = xall[0].reshape(D, S)
    bias = jnp.broadcast_to(b_in[...], (128, H)).T
    acc = dot(w_in[...], x_full, 0, 0)
    acc = acc + jnp.concatenate([bias] * (S // 128), axis=1) if S >= 128 else acc + bias[:, :S]
    t = jnp.tanh(ROOT * (acc + 0.044715 * acc * acc * acc))
    hid[...] = (0.5 * acc * (1.0 + t)).astype(BF)
    dgelu[...] = 0.5 * (1.0 + t) + 0.5 * acc * (1.0 - t * t) * (ROOT * (1.0 + 3 * 0.044715 * acc * acc))
    relay(1)

    @functools.cache
    def half_copies(way):
        return [
            remote(xhalf.at[way, 0], rhalf.at[way, 0], r_send.at[way, 0], r_recv.at[way, 0], at("rep", left_x)),
            remote(xhalf.at[way, 1], rhalf.at[way, 1], r_send.at[way, 1], r_recv.at[way, 1], at("rep", right_x)),
        ]

    @functools.cache
    def full_copies(way):
        return [
            remote(xfull.at[way, 0], rfull.at[way, 0], r_send.at[way, 2], r_recv.at[way, 2], at("rep", left_x)),
            remote(xfull.at[way, 1], rfull.at[way, 1], r_send.at[way, 3], r_recv.at[way, 3], at("rep", right_x)),
        ]

    def partial(way, target):
        span = pl.ds(pl.multiple_of(target * F, F), F)
        return dot(w_out_t[span, :], hid[...], 1, 0) if way == 0 else dot(w_in[span, :], d_pre[...], 1, 0)

    def scatter_start(way):
        far = partial(way, far_x).astype(BF)
        xhalf[way, 0] = far[0:HF]
        xhalf[way, 1] = far[HF:F]
        start(half_copies(way))

    def scatter_middle(way):
        halves = half_copies(way)
        for i, target in ((0, left_x), (1, right_x)):
            mine = partial(way, target)
            halves[i].wait_recv()
            came = rhalf[way, i].astype(F32)
            if i == 0:
                xfull[way, i] = jnp.concatenate([mine[0:HF] + came, mine[HF:F]], axis=0).astype(BF)
            else:
                xfull[way, i] = jnp.concatenate([mine[0:HF], mine[HF:F] + came], axis=0).astype(BF)
            start([full_copies(way)[i]])

    def scatter_end(way):
        total = partial(way, r)
        for i, copy in enumerate(full_copies(way)):
            copy.wait_recv()
            total = total + rfull[way, i].astype(F32)
        return total

    @functools.cache
    def b_copies(way):
        return [
            remote(
                back.at[way, lax.rem(g + j, G)], yret.at[way, :, g],
                b_send.at[way, j - 1], b_recv.at[way, j - 1], at("grp", lax.rem(g + j, G)),
            )
            for j in range(1, G)
        ]

    def give_back(way, total):
        rows_of = G * Q
        value = total.astype(BF)
        low = jnp.concatenate([value[128:F, h * rows_of : (h + 1) * rows_of] for h in range(2)], axis=0)
        pieces = [value[0:128, h * rows_of : (h + 1) * rows_of] for h in range(2)] + [low]
        for i, piece in enumerate(pieces):
            back[way, :, i] = piece.T.reshape(G, Q, 128)
        start(b_copies(way))
        yret[way, :, g] = back[way, g]

    scatter_start(0)
    arrive(1)
    g_full = xall[1].reshape(D, S)
    slope = dot(w_out[...], g_full, 1, 0)
    d_pre[...] = (slope * dgelu[...]).astype(BF)
    scatter_middle(0)
    scatter_start(1)
    out_bias = jnp.broadcast_to(b_out[...], (128, F)).T
    wide = jnp.concatenate([out_bias] * (S // 128), axis=1) if S >= 128 else out_bias[:, :S]
    give_back(0, scatter_end(0) + wide)
    scatter_middle(1)

    @functools.cache
    def s_copies(way, i):
        found = []
        for side, peer in ((0, right_z), (1, left_z)):
            src, dst = zs.at[way, side, i], zr.at[way, side, i]
            if i == 0:
                span = pl.ds(side * HF, HF)
                src, dst = src.at[span], dst.at[span]
            found.append(remote(src, dst, s_send.at[way, side, i], s_recv.at[way, side, i], at("node", peer)))
        return found

    @functools.cache
    def m_copies(i):
        return [
            remote(gs.at[side, i], gr.at[side, i], s_send.at[2, side, i], s_recv.at[2, side, i], at("node", peer))
            for side, peer in ((0, right_z), (1, left_z))
        ]

    def returned(way, u):
        h, v = u // V, u % V
        a = yret[way, h, :, v * 8 : v * 8 + 8, :].reshape(G * 8, 128)
        b = yret[way, 2, :, v * 8 : v * 8 + 8, :].reshape(G * 8, 128)
        both = jnp.concatenate([a, b], axis=1)
        if way == 0:
            hot = [onehot[u, 0], onehot[u, 1]]
        else:
            hot = [onehot[u, 0] + onehot[u, 1]]
        results = []
        for one in hot:
            full = dot(both, one, 0, 0)
            results.append(jnp.concatenate([full[0:128], full[128 + h * FB : 128 + (h + 1) * FB]], axis=0))
        out = []
        for p, slot in enumerate(pair(u)):
            cut = [one[:, p * T : (p + 1) * T] for one in results]
            if way == 1:
                out.append((cut[0], None))
                continue
            info = zm[slot]
            sent = (cot[...] if slot == 0 else zc[slot]).astype(F32)
            value = info[2:3, :] * cut[0] + info[3:4, :] * cut[1]
            sums = [jnp.sum(one * sent, axis=0, keepdims=True) for one in cut]
            out.append((value, jnp.concatenate(sums + [jnp.zeros((6, T), F32)], axis=0)))
        return out

    def ring(way):
        (home, home_g), (value, sums) = returned(way, U - 1)
        for side in range(2):
            zs[way, side, 0] = value.astype(BF)
        start(s_copies(way, 0))
        if way == 0:
            gs[0, 0] = sums
            gs[1, 0] = jnp.zeros((8, T), F32)
            start(m_copies(0))
        for i in range(1, U):
            ahead, behind = returned(way, U - 1 - i)
            before = s_copies(way, i - 1)
            for side, (value, sums) in enumerate((ahead, behind)):
                before[side].wait_recv()
                came = zr[way, side, i - 1]
                if i == 1:
                    came = came.astype(F32)
                    lo, hi = value[0:HF], value[HF:F]
                    if side == 0:
                        total = jnp.concatenate([lo + came[0:HF], hi], axis=0)
                    else:
                        total = jnp.concatenate([lo, hi + came[HF:F]], axis=0)
                else:
                    total = value + came.astype(F32)
                zs[way, side, i] = total.astype(BF)
                start([s_copies(way, i)[side]])
                if way == 0:
                    m_copies(i - 1)[side].wait_recv()
                    gs[side, i] = sums + gr[side, i - 1]
                    start([m_copies(i)[side]])
        last = s_copies(way, U - 1)
        total = home
        for side in range(2):
            last[side].wait_recv()
            total = total + zr[way, side, U - 1].astype(F32)
            if way == 0:
                m_copies(U - 1)[side].wait_recv()
                home_g = home_g + gr[side, U - 1]
        return total, home_g

    for copy in b_copies(0):
        copy.wait_recv()
    total, sums = ring(0)
    mixed[...] = total.astype(BF)
    dsum[...] = sums
    shares = [
        remote(dsum, drecv.at[j - 1], p_send.at[j - 1], p_recv.at[j - 1], at("rep", lax.rem(r + j, R)))
        for j in range(1, R)
    ]
    start(shares)

    give_back(1, scatter_end(1))

    ones = jnp.ones((8, S), BF)
    d_w_in[...] = dot(xall[0].reshape(D, S), d_pre[...], 1, 1)
    d_w_out[...] = dot(hid[...], xall[1].reshape(D, S), 1, 1)
    d_b_in[...] = dot(ones, d_pre[...], 1, 1)[0:1]
    d_b_out[...] = dot(ones, xall[1, r], 1, 1)[0:1]

    for copy in b_copies(1):
        copy.wait_recv()
    total, _ = ring(1)
    d_tok[...] = total.astype(BF)
    for j, copy in enumerate(shares):
        copy.wait_recv()
        sums = sums + drecv[j]
    d_gates[...] = sums[0:2]
    for copy in started:
        copy.wait_send()


def per_device(tokens, gates, expert_ids, w_in, b_in, w_out, b_out, cotangent):
    N, G, R = lax.axis_size("node"), lax.axis_size("grp"), lax.axis_size("rep")
    T, F = tokens.shape
    _, D, H = w_in.shape
    U = N // 2
    V = U // 2
    Q = V * 8
    S = 2 * G * Q
    HF = F // 2
    dma = pltpu.SemaphoreType.DMA
    vmem = pl.BlockSpec(memory_space=pltpu.VMEM)
    out = pl.pallas_call(
        functools.partial(fused, N, G, R),
        out_shape=(
            jax.ShapeDtypeStruct((F, T), BF),
            jax.ShapeDtypeStruct((F, T), BF),
            jax.ShapeDtypeStruct((2, T), F32),
            jax.ShapeDtypeStruct((D, H), F32),
            jax.ShapeDtypeStruct((1, H), F32),
            jax.ShapeDtypeStruct((H, D), F32),
            jax.ShapeDtypeStruct((1, F), F32),
        ),
        in_specs=[vmem] * 8,
        out_specs=(vmem,) * 7,
        scratch_shapes=[
            pltpu.VMEM((N, F, T), BF),
            pltpu.VMEM((N, F, T), BF),
            pltpu.VMEM((N, 8, T), F32),
            pltpu.VMEM((U, 2, G * 8, 2 * T), BF),
            pltpu.VMEM((2, G, 3, Q, 128), BF),
            pltpu.VMEM((2, 3, G, Q, 128), BF),
            pltpu.VMEM((2, R, F, S), BF),
            pltpu.VMEM((D, H), BF),
            pltpu.VMEM((8, 128), F32),
            pltpu.VMEM((H, S), F32),
            pltpu.VMEM((H, S), BF),
            pltpu.VMEM((H, S), BF),
            pltpu.VMEM((2, 2, HF, S), BF),
            pltpu.VMEM((2, 2, F, S), BF),
            pltpu.VMEM((2, 2, HF, S), BF),
            pltpu.VMEM((2, 2, F, S), BF),
            pltpu.VMEM((2, G, 3, Q, 128), BF),
            pltpu.VMEM((2, 3, G, Q, 128), BF),
            pltpu.VMEM((2, 2, U, F, T), BF),
            pltpu.VMEM((2, 2, U, F, T), BF),
            pltpu.VMEM((2, U, 8, T), F32),
            pltpu.VMEM((2, U, 8, T), F32),
            pltpu.VMEM((8, T), F32),
            pltpu.VMEM((R - 1, 8, T), F32),
            dma((3, 2, U)),
            dma((3, 2, U)),
            dma((2, G - 1)),
            dma((2, G - 1)),
            dma((2, 4)),
            dma((2, 4)),
            dma((2, 4)),
            dma((2, 4)),
            dma((2, G - 1)),
            dma((2, G - 1)),
            dma((3, 2, U)),
            dma((3, 2, U)),
            dma((R - 1,)),
            dma((R - 1,)),
        ],
        compiler_params=pltpu.CompilerParams(
            collective_id=0, has_side_effects=True, vmem_limit_bytes=60 * 2**20
        ),
    )(
        tokens.T, cotangent.T, expert_ids.T, gates.T,
        w_in[0], b_in, w_out[0], b_out,
    )
    mixed, d_tok, d_gates, d_w_in, d_b_in, d_w_out, d_b_out = out
    return (mixed.T, d_tok.T, d_gates.T, d_w_in[None], d_b_in, d_w_out[None], d_b_out)


def solution(mesh):
    both = ("node", "grp")
    return jax.shard_map(
        per_device,
        mesh=mesh,
        in_specs=(
            P(both, "rep"),
            P(both, None),
            P(both, None),
            P(both, None, "rep"),
            P(both, "rep"),
            P(both, "rep", None),
            P(both, "rep"),
            P(both, "rep"),
        ),
        out_specs=(
            P(both, "rep"),
            P(both, "rep"),
            P(both, None),
            P(both, None, "rep"),
            P(both, "rep"),
            P(both, "rep", None),
            P(both, "rep"),
        ),
        check_vma=False,
    )
```

time: 197 us -> 155 us (0.79)
  the two profiles are of different devices: /device:TPU:1 before, /device:TPU:32 now
where the time goes in v1:
time: 155 us
  Pallas kernels  146 us (94%)
  local copies, waits for them, and re-layouts  8.63 us (6%)
    pallas_call x1, Pallas kernels, per_device(): pl.pallas_call(functools.partial(fused, N, G, R), out_shape=(jax.ShapeDty...  146 us
    unnamed x13, local copies, waits for them, and re-layouts  8.63 us

profile of v1, /device:TPU:32, one launch (start us, length us, event | category | flops | bytes accessed | tf_op | source)
XLA Modules:
  0.0 154.8 jit_solution(9022921116727833127)
XLA Ops:
  0.6 145.5 %shard_map.135 = (bf16[192,128]{1,0:T(8,128)(2,1)}, bf16[192,128]{1,0:T(8,128)(2,1)}, f32[2,128]{1,0:T(2,128)}, f32[768,384]{1,0:T(8,128)}, f32[1,384]{1,0:T(1,1...) custom-call(bf16[192,128]{1,0:T(8,128)(2,1)} %bitcast.15, bf16[192,128]{1,0:T(8,128)(2,1)} %bitcast.16, s32[2,128]{1,0:T(2,128)} %bitcast.19, ...), custom_call_target="tpu_custom_call" | custom-call | tf_op jit(solution)/shard_map/pallas_call | solution.py:420
  146.2 1.4 copy.22
  147.6 1.4 copy.23
  149.0 1.2 copy.24
  150.2 0.0 copy-start.1
  150.2 0.0 copy-start
  150.2 2.5 %copy.25 = f32[1,768,384]{2,1,0:T(8,128)} copy(f32[1,768,384]{2,1,0:T(8,128)} %bitcast.12) | data formatting | bytes 2359296
  152.6 0.0 copy-done.1
  152.6 0.6 copy.26
  153.2 0.0 copy-done
  153.2 0.0 copy-start.2
  153.2 1.0 copy.27
  154.2 0.0 copy-done.2
  154.2 0.6 copy.28
Async XLA Ops:
  150.2 2.5 %copy-start.1 = (f32[1,384]{1,0:T(1,128)S(1)}, f32[1,384]{1,0:T(1,128)}, u32[]{:S(2)}) copy-start(f32[1,384]{1,0:T(1,128)} %get-tuple-element.32) | copy-start | bytes 4612
  150.2 3.0 %copy-start = (f32[384,768]{1,0:T(8,128)S(1)}, f32[384,768]{1,0:T(8,128)}, u32[]{:S(2)}) copy-start(f32[384,768]{1,0:T(8,128)} %get-tuple-element.19) | copy-start | bytes 3538948
  153.2 1.0 copy-start.2

commit v2 on v1

v2 whole, which is shorter than its diff:
```python
import functools
import math

import jax
import jax.numpy as jnp
from jax import lax
from jax.experimental import pallas as pl
from jax.experimental.pallas import tpu as pltpu
from jax.sharding import PartitionSpec as P

MESH = pl.DeviceIdType.MESH
CAP = 4
BF = jnp.bfloat16
F32 = jnp.float32
ROOT = math.sqrt(2.0 / math.pi)


def dot(a, b, ca, cb):
    return lax.dot_general(a, b, (((ca,), (cb,)), ((), ())), preferred_element_type=F32)


def fused(
    N, G, R,
    tok, cot, ids, gates, w_in, b_in, w_out, b_out,
    mixed, d_tok, d_gates, d_w_in, d_b_in, d_w_out, d_b_out,
    zsend, zrecv, place, ysend, yrecv, xall, w_out_t, dgelu, hid, d_pre,
    xhalf, xfull, rhalf, rfull, back, yret, zback, zret, grad_in, grad_out, dsum, drecv,
    z_send, z_recv, y_send, y_recv, x_send, x_recv, r_send, r_recv,
    b_send, b_recv, s_send, s_recv, p_send, p_recv, o_sem,
):
    n, g, r = lax.axis_index("node"), lax.axis_index("grp"), lax.axis_index("rep")
    F, T = tok.shape
    D, H = w_in.shape
    A = G * CAP
    B = A // 2
    K = N // 4
    Q = 2 * N
    S = 2 * G * Q
    HF, FB = F // 2, F - 128
    C = G // 2

    right_x, left_x = lax.rem(r + 1, R), lax.rem(r + R - 1, R)
    far_x = lax.rem(r + 2, R)

    barrier = pltpu.get_barrier_semaphore()
    peers = [{"node": lax.rem(n + j, N)} for j in range(1, N)]
    peers += [{"grp": lax.rem(g + j, G)} for j in range(1, G)]
    peers += [{"rep": lax.rem(r + j, R)} for j in range(1, R)]
    for peer in peers:
        pl.semaphore_signal(barrier, inc=1, device_id=peer, device_id_type=MESH)

    def remote(src, dst, send, recv, peer):
        return pltpu.make_async_remote_copy(
            src_ref=src, dst_ref=dst, send_sem=send, recv_sem=recv,
            device_id=peer, device_id_type=MESH,
        )

    started = []

    def start(copies):
        for copy in copies:
            copy.start()
        started.extend(copies)

    def arrived(copies):
        for copy in copies:
            copy.wait_recv()

    ids_f = ids[...].astype(F32)
    rows = [ids_f[k : k + 1, :] for k in range(2)]
    cols = [jnp.broadcast_to(row, (T, T)).T for row in rows]
    earlier = lax.broadcasted_iota(jnp.int32, (T, T), 0) < lax.broadcasted_iota(jnp.int32, (T, T), 1)
    slot = lax.broadcasted_iota(jnp.int32, (N * A, T), 0).astype(F32)
    for k in range(2):
        same = jnp.where(cols[0] == rows[k], 1.0, 0.0) + jnp.where(cols[1] == rows[k], 1.0, 0.0)
        rank = jnp.sum(jnp.where(earlier, same, 0.0), axis=0, keepdims=True)
        target = rows[k] * CAP + rank
        place[:, k * T : (k + 1) * T] = jnp.where(slot == target, 1.0, 0.0).astype(BF)

    order = [N // 2]
    for j in range(N // 2 - 1, 0, -1):
        order += [j, N - j]

    @functools.cache
    def z_copies(which):
        return [
            remote(
                zsend.at[which, lax.rem(n + j, N)], zrecv.at[which, n],
                z_send.at[which, j - 1], z_recv.at[which, j - 1], {"node": lax.rem(n + j, N)},
            )
            for j in order
        ]

    def lay(which):
        if which == 0:
            got = dot(place[:, 0:T] + place[:, T : 2 * T], tok[...], 1, 1)
        else:
            wide = cot[...].astype(F32)
            grads = [(gates[k : k + 1, :] * wide).astype(BF) for k in range(2)]
            got = dot(place[...], jnp.concatenate(grads, axis=1), 1, 1)
        got = got.reshape(N, A, F)
        zsend[which, :, 0:A, :] = got[:, :, 0:128].astype(BF)
        for c in range(2):
            zsend[which, :, A : A + B, c * FB : (c + 1) * FB] = got[:, c * B : (c + 1) * B, 128:F].astype(BF)

    lay(0)
    pl.semaphore_wait(barrier, len(peers))
    start(z_copies(0))
    lay(1)
    start(z_copies(1))
    for which in range(2):
        zrecv[which, n] = zsend[which, n]

    def shuffle(experts):
        size = 4 * experts * CAP
        i = lax.broadcasted_iota(jnp.int32, (size, size), 0)
        j = lax.broadcasted_iota(jnp.int32, (size, size), 1)
        e, v, s = i // (4 * CAP), lax.rem(i // CAP, 4), lax.rem(i, CAP)
        return jnp.where(j == (v * experts + e) * CAP + s, 1.0, 0.0).astype(BF)

    mix_a, mix_b = shuffle(G), shuffle(C)

    @functools.cache
    def y_copies(which):
        return [
            remote(
                ysend.at[which, lax.rem(g + j, G)], yrecv.at[which, :, g],
                y_send.at[which, j - 1], y_recv.at[which, j - 1], {"grp": lax.rem(g + j, G)},
            )
            for j in range(1, G)
        ]

    def regroup(which):
        for q in range(K):
            h, w = q // (K // 2), q % (K // 2)
            span = slice(w * 16, w * 16 + 16)
            a = zrecv[which, 4 * q : 4 * q + 4, 0:A, :].reshape(4 * A, 128)
            ysend[which, :, h, span, :] = dot(mix_a, a, 1, 0).astype(BF).reshape(G, 16, 128)
            b = dot(mix_b, zrecv[which, 4 * q : 4 * q + 4, A : A + B, :].reshape(4 * B, 128), 1, 0)
            turned = pltpu.roll(b, FB, 1)
            for c in range(2):
                piece = (b if c == h else turned)[:, h * FB : (h + 1) * FB]
                ysend[which, c * C : (c + 1) * C, 2, span, h * FB : (h + 1) * FB] = (
                    piece.astype(BF).reshape(C, 16, FB)
                )
        start(y_copies(which))
        yrecv[which, :, g] = ysend[which, g]

    @functools.cache
    def x_near(which):
        own = xall.at[which, r]
        return [
            remote(own, own, x_send.at[which, 0], x_recv.at[which, 0], {"rep": right_x}),
            remote(own, own, x_send.at[which, 1], x_recv.at[which, 1], {"rep": left_x}),
        ]

    @functools.cache
    def x_relay(which):
        top = xall.at[which, left_x, pl.ds(0, HF)]
        low = xall.at[which, right_x, pl.ds(HF, HF)]
        return [
            remote(top, top, x_send.at[which, 2], x_recv.at[which, 2], {"rep": right_x}),
            remote(low, low, x_send.at[which, 3], x_recv.at[which, 3], {"rep": left_x}),
        ]

    def unpack(which):
        rows_of = G * Q
        arrived(y_copies(which))
        for h in range(2):
            xall[which, r, 0:128, h * rows_of : (h + 1) * rows_of] = (
                yrecv[which, h].reshape(rows_of, 128).T
            )
        low = yrecv[which, 2].reshape(rows_of, 128).T
        for h in range(2):
            xall[which, r, 128:F, h * rows_of : (h + 1) * rows_of] = low[h * FB : (h + 1) * FB]
        start(x_near(which))

    def relay(which):
        near, passed = x_near(which), x_relay(which)
        for i in range(2):
            near[i].wait_recv()
            start([passed[i]])

    w_out_t[...] = w_out[...].T
    bias = jnp.broadcast_to(b_in[...], (128, H)).T
    out_bias = jnp.broadcast_to(b_out[...], (128, F)).T

    def widen(column):
        return jnp.concatenate([column] * (S // 128), axis=1) if S >= 128 else column[:, :S]

    @functools.cache
    def half_copies(way):
        return [
            remote(xhalf.at[way, 0], rhalf.at[way, 0], r_send.at[way, 0], r_recv.at[way, 0], {"rep": left_x}),
            remote(xhalf.at[way, 1], rhalf.at[way, 1], r_send.at[way, 1], r_recv.at[way, 1], {"rep": right_x}),
        ]

    @functools.cache
    def full_copies(way):
        return [
            remote(xfull.at[way, 0], rfull.at[way, 0], r_send.at[way, 2], r_recv.at[way, 2], {"rep": left_x}),
            remote(xfull.at[way, 1], rfull.at[way, 1], r_send.at[way, 3], r_recv.at[way, 3], {"rep": right_x}),
        ]

    def partial(way, target):
        span = pl.ds(pl.multiple_of(target * F, F), F)
        return dot(w_out_t[span, :], hid[...], 1, 0) if way == 0 else dot(w_in[span, :], d_pre[...], 1, 0)

    def scatter_start(way):
        far = partial(way, far_x).astype(BF)
        xhalf[way, 0] = far[0:HF]
        xhalf[way, 1] = far[HF:F]
        start(half_copies(way))

    def scatter_middle(way):
        for i, target in ((0, left_x), (1, right_x)):
            mine = partial(way, target)
            half_copies(way)[i].wait_recv()
            came = rhalf[way, i].astype(F32)
            if i == 0:
                xfull[way, i] = jnp.concatenate([mine[0:HF] + came, mine[HF:F]], axis=0).astype(BF)
            else:
                xfull[way, i] = jnp.concatenate([mine[0:HF], mine[HF:F] + came], axis=0).astype(BF)
            start([full_copies(way)[i]])

    @functools.cache
    def b_copies(way):
        return [
            remote(
                back.at[way, lax.rem(g + j, G)], yret.at[way, :, g],
                b_send.at[way, j - 1], b_recv.at[way, j - 1], {"grp": lax.rem(g + j, G)},
            )
            for j in range(1, G)
        ]

    def scatter_end(way):
        rows_of = G * Q
        total = partial(way, r)
        if way == 0:
            total = total + widen(out_bias)
        for i, copy in enumerate(full_copies(way)):
            copy.wait_recv()
            total = total + rfull[way, i].astype(F32)
        value = total.astype(BF)
        low = jnp.concatenate([value[128:F, h * rows_of : (h + 1) * rows_of] for h in range(2)], axis=0)
        pieces = [value[0:128, h * rows_of : (h + 1) * rows_of] for h in range(2)] + [low]
        for i, piece in enumerate(pieces):
            back[way, :, i] = piece.T.reshape(G, Q, 128)
        start(b_copies(way))
        yret[way, :, g] = back[way, g]

    @functools.cache
    def s_copies(way):
        return [
            remote(
                zback.at[way, lax.rem(n + j, N)], zret.at[way, n],
                s_send.at[way, j - 1], s_recv.at[way, j - 1], {"node": lax.rem(n + j, N)},
            )
            for j in order
        ]

    def ungroup(way):
        arrived(b_copies(way))
        for q in range(K):
            h, w = q // (K // 2), q % (K // 2)
            span = slice(w * 16, w * 16 + 16)
            a = yret[way, h, :, span, :].reshape(4 * A, 128)
            zback[way, 4 * q : 4 * q + 4, 0:A, :] = dot(mix_a, a, 0, 0).astype(BF).reshape(4, A, 128)
            b = yret[way, 2, :, span, :].reshape(4 * A, 128)
            for c in range(2):
                part = dot(mix_b, b[c * 4 * B : (c + 1) * 4 * B], 0, 0)
                if c != h:
                    part = pltpu.roll(part, FB, 1)
                zback[way, 4 * q : 4 * q + 4, A : A + B, c * FB : (c + 1) * FB] = (
                    part[:, c * FB : (c + 1) * FB].astype(BF).reshape(4, B, FB)
                )
        start(s_copies(way))
        zret[way, n] = zback[way, n]

    def landed(way):
        arrived(s_copies(way))
        hot = place[...] if way == 0 else place[:, 0:T] + place[:, T : 2 * T]
        a = zret[way, :, 0:A, :].reshape(N * A, 128)
        b = zret[way, :, A : A + B, :].reshape(N * B, 128)
        top = dot(a, hot, 0, 0)
        hot = hot.reshape(N, 2, B, hot.shape[1])
        low = [dot(b, hot[:, c].reshape(N * B, hot.shape[3]), 0, 0)[c * FB : (c + 1) * FB] for c in range(2)]
        return jnp.concatenate([top, low[0] + low[1]], axis=0)

    arrived(z_copies(0))
    regroup(0)
    unpack(0)
    relay(0)
    arrived(z_copies(1))
    regroup(1)
    arrived(x_relay(0))
    acc = dot(w_in[...], xall[0].reshape(D, S), 0, 0) + widen(bias)
    t = jnp.tanh(ROOT * (acc + 0.044715 * acc * acc * acc))
    hid[...] = (0.5 * acc * (1.0 + t)).astype(BF)
    dgelu[...] = 0.5 * (1.0 + t) + 0.5 * acc * (1.0 - t * t) * (ROOT * (1.0 + 3 * 0.044715 * acc * acc))
    unpack(1)
    scatter_start(0)
    relay(1)
    scatter_middle(0)
    arrived(x_relay(1))
    slope = dot(w_out[...], xall[1].reshape(D, S), 1, 0)
    d_pre[...] = (slope * dgelu[...]).astype(BF)
    scatter_start(1)
    scatter_end(0)
    scatter_middle(1)
    ungroup(0)
    scatter_end(1)

    ones = jnp.ones((8, S), BF)
    grad_in[...] = dot(xall[0].reshape(D, S), d_pre[...], 1, 1)
    grad_out[...] = dot(hid[...], xall[1].reshape(D, S), 1, 1)
    outs = [
        pltpu.make_async_copy(grad_in, d_w_in, o_sem.at[0]),
        pltpu.make_async_copy(grad_out, d_w_out, o_sem.at[1]),
    ]
    for copy in outs:
        copy.start()
    d_b_in[...] = dot(ones, d_pre[...], 1, 1)[0:1]
    d_b_out[...] = dot(ones, xall[1, r], 1, 1)[0:1]

    ungroup(1)
    both = landed(0)
    wide = cot[...].astype(F32)
    cut = [both[:, k * T : (k + 1) * T] for k in range(2)]
    mixed[...] = (gates[0:1, :] * cut[0] + gates[1:2, :] * cut[1]).astype(BF)
    sums = [jnp.sum(one * wide, axis=0, keepdims=True) for one in cut]
    sums = jnp.concatenate(sums + [jnp.zeros((6, T), F32)], axis=0)
    dsum[...] = sums
    shares = [
        remote(dsum, drecv.at[j - 1], p_send.at[j - 1], p_recv.at[j - 1], {"rep": lax.rem(r + j, R)})
        for j in range(1, R)
    ]
    start(shares)
    d_tok[...] = landed(1).astype(BF)
    arrived(shares)
    for j in range(R - 1):
        sums = sums + drecv[j]
    d_gates[...] = sums[0:2]
    for copy in outs:
        copy.wait()
    for copy in started:
        copy.wait_send()


def hand_out(*refs):
    count = len(refs) // 3
    sources, results, held = refs[:count], refs[count : 2 * count], refs[2 * count : 3 * count]
    sem_in, sem_out = refs[3 * count :]
    inward = [pltpu.make_async_copy(s, h, sem_in.at[i]) for i, (s, h) in enumerate(zip(sources, held))]
    outward = [pltpu.make_async_copy(h, o, sem_out.at[i]) for i, (h, o) in enumerate(zip(held, results))]
    for copy in inward:
        copy.start()
    for i, copy in enumerate(inward):
        copy.wait()
        outward[i].start()
    for copy in outward:
        copy.wait()


def per_device(tokens, gates, expert_ids, w_in, b_in, w_out, b_out, cotangent):
    N, G, R = lax.axis_size("node"), lax.axis_size("grp"), lax.axis_size("rep")
    T, F = tokens.shape
    _, D, H = w_in.shape
    A, B, Q = G * CAP, G * CAP // 2, 2 * N
    S = 2 * G * Q
    HF = F // 2
    dma = pltpu.SemaphoreType.DMA
    vmem = pl.BlockSpec(memory_space=pltpu.VMEM)
    any_ = pl.BlockSpec(memory_space=pl.ANY)
    shapes = (
        jax.ShapeDtypeStruct((F, T), BF),
        jax.ShapeDtypeStruct((F, T), BF),
        jax.ShapeDtypeStruct((2, T), F32),
        jax.ShapeDtypeStruct((D, H), F32),
        jax.ShapeDtypeStruct((1, H), F32),
        jax.ShapeDtypeStruct((H, D), F32),
        jax.ShapeDtypeStruct((1, F), F32),
    )
    out = pl.pallas_call(
        functools.partial(fused, N, G, R),
        out_shape=shapes,
        in_specs=[vmem] * 8,
        out_specs=(vmem, vmem, vmem, any_, vmem, any_, vmem),
        scratch_shapes=[
            pltpu.VMEM((2, N, A + B, 128), BF),
            pltpu.VMEM((2, N, A + B, 128), BF),
            pltpu.VMEM((N * A, 2 * T), BF),
            pltpu.VMEM((2, G, 3, Q, 128), BF),
            pltpu.VMEM((2, 3, G, Q, 128), BF),
            pltpu.VMEM((2, R, F, S), BF),
            pltpu.VMEM((D, H), BF),
            pltpu.VMEM((H, S), F32),
            pltpu.VMEM((H, S), BF),
            pltpu.VMEM((H, S), BF),
            pltpu.VMEM((2, 2, HF, S), BF),
            pltpu.VMEM((2, 2, F, S), BF),
            pltpu.VMEM((2, 2, HF, S), BF),
            pltpu.VMEM((2, 2, F, S), BF),
            pltpu.VMEM((2, G, 3, Q, 128), BF),
            pltpu.VMEM((2, 3, G, Q, 128), BF),
            pltpu.VMEM((2, N, A + B, 128), BF),
            pltpu.VMEM((2, N, A + B, 128), BF),
            pltpu.VMEM((D, H), F32),
            pltpu.VMEM((H, D), F32),
            pltpu.VMEM((8, T), F32),
            pltpu.VMEM((R - 1, 8, T), F32),
            dma((2, N - 1)),
            dma((2, N - 1)),
            dma((2, G - 1)),
            dma((2, G - 1)),
            dma((2, 4)),
            dma((2, 4)),
            dma((2, 4)),
            dma((2, 4)),
            dma((2, G - 1)),
            dma((2, G - 1)),
            dma((2, N - 1)),
            dma((2, N - 1)),
            dma((R - 1,)),
            dma((R - 1,)),
            dma((2,)),
        ],
        compiler_params=pltpu.CompilerParams(
            collective_id=0, has_side_effects=True, vmem_limit_bytes=60 * 2**20
        ),
    )(
        tokens.T, cotangent.T, expert_ids.T, gates.T,
        w_in[0], b_in, w_out[0], b_out,
    )
    out = pl.pallas_call(
        hand_out,
        out_shape=shapes,
        in_specs=[any_] * 7,
        out_specs=(any_,) * 7,
        scratch_shapes=[pltpu.VMEM(one.shape, one.dtype) for one in shapes] + [dma((7,)), dma((7,))],
    )(*out)
    mixed, d_tok, d_gates, d_w_in, d_b_in, d_w_out, d_b_out = out
    return (mixed.T, d_tok.T, d_gates.T, d_w_in[None], d_b_in, d_w_out[None], d_b_out)


def solution(mesh):
    both = ("node", "grp")
    return jax.shard_map(
        per_device,
        mesh=mesh,
        in_specs=(
            P(both, "rep"),
            P(both, None),
            P(both, None),
            P(both, None, "rep"),
            P(both, "rep"),
            P(both, "rep", None),
            P(both, "rep"),
            P(both, "rep"),
        ),
        out_specs=(
            P(both, "rep"),
            P(both, "rep"),
            P(both, None),
            P(both, None, "rep"),
            P(both, "rep"),
            P(both, "rep", None),
            P(both, "rep"),
        ),
        check_vma=False,
    )
```

time: 155 us -> 95.8 us (0.62)
  the two profiles are of different devices: /device:TPU:32 before, /device:TPU:1 now
where the time goes in v2:
time: 95.8 us; the launch traced here: 95.6 us
  Pallas kernels  94.9 us (99%)
    pallas_call x1, Pallas kernels, per_device(): pl.pallas_call(functools.partial(fused, N, G, R), out_shape=shapes, in_sp...  92.1 us
    pallas_call x1, Pallas kernels, per_device(): pl.pallas_call(hand_out, out_shape=shapes, in_specs=[any_] * 7, out_specs...  2.86 us

profile of v2, /device:TPU:1, one launch (start us, length us, event | category | flops | bytes accessed | tf_op | source)
XLA Modules:
  0.0 95.6 jit_solution(18431554899406024412)
XLA Ops:
  0.6 92.1 %shard_map.135 = (bf16[192,128]{1,0:T(8,128)(2,1)}, bf16[192,128]{1,0:T(8,128)(2,1)}, f32[2,128]{1,0:T(2,128)}, f32[768,384]{1,0:T(8,128)}, f32[1,384]{1,0:T(1,1...) custom-call(bf16[192,128]{1,0:T(8,128)(2,1)} %bitcast.13, bf16[192,128]{1,0:T(8,128)(2,1)} %bitcast.14, s32[2,128]{1,0:T(2,128)} %bitcast.15, ...), custom_call_target="tpu_custom_call" | custom-call | tf_op jit(solution)/shard_map/pallas_call | solution.py:384
  92.7 2.9 %shard_map.136 = (bf16[192,128]{1,0:T(8,128)(2,1)}, bf16[192,128]{1,0:T(8,128)(2,1)}, f32[2,128]{1,0:T(2,128)}, f32[768,384]{1,0:T(8,128)}, f32[1,384]{1,0:T(1,1...) custom-call(bf16[192,128]{1,0:T(8,128)(2,1)} %get-tuple-element.21.refs_0_, bf16[192,128]{1,0:T(8,128)(2,1)} %get-tuple-element.22.refs_1_, ...), custom_call_target="tpu_custom_call" | custom-call | tf_op jit(solution)/shard_map/pallas_call | solution.py:435

commit v3 on v2

v3 whole, which is shorter than its diff:
```python
import functools
import math

import jax
import jax.numpy as jnp
from jax import lax
from jax.experimental import pallas as pl
from jax.experimental.pallas import tpu as pltpu
from jax.sharding import PartitionSpec as P

MESH = pl.DeviceIdType.MESH
CAP = 4
BF = jnp.bfloat16
F32 = jnp.float32
ROOT = math.sqrt(2.0 / math.pi)


def dot(a, b, ca, cb):
    return lax.dot_general(a, b, (((ca,), (cb,)), ((), ())), preferred_element_type=F32)


def fused(
    N, G, R,
    tok, cot, ids, gates, w_in_hbm, b_in, w_out_hbm, b_out,
    mixed, d_tok, d_gates, d_w_in, d_b_in, d_w_out, d_b_out,
    place, ysend, yrecv, zsend, zrecv, xall, w_in, w_out, w_out_t, dgelu, hid, d_pre,
    xhalf, xfull, rhalf, rfull, zback, zret, back, yret, grad_in, grad_out, dsum, drecv,
    y_send, y_recv, z_send, z_recv, x_send, x_recv, r_send, r_recv,
    s_send, s_recv, b_send, b_recv, p_send, p_recv, o_sem, reach,
):
    n, g, r = lax.axis_index("node"), lax.axis_index("grp"), lax.axis_index("rep")
    F, T = tok.shape
    D, H = w_in.shape
    A = G * CAP
    B = A // 2
    K = N // 4
    M = N // 2
    Q = 2 * N
    W = M * B
    HF, FB = F // 2, F - 128
    C = G // 2

    right_x, left_x = lax.rem(r + 1, R), lax.rem(r + R - 1, R)
    far_x = lax.rem(r + 2, R)

    barrier = pltpu.get_barrier_semaphore()
    peers = [{"node": lax.rem(n + j, N)} for j in (1, N - 1)]
    peers += [{"grp": lax.rem(g + j, G)} for j in range(1, G)]
    peers += [{"rep": lax.rem(r + j, R)} for j in range(1, R)]
    for peer in peers:
        pl.semaphore_signal(barrier, inc=1, device_id=peer, device_id_type=MESH)

    weights = [
        pltpu.make_async_copy(w_in_hbm, w_in, o_sem.at[2]),
        pltpu.make_async_copy(w_out_hbm, w_out, o_sem.at[3]),
    ]
    for copy in weights:
        copy.start()

    def remote(src, dst, send, recv, peer):
        return pltpu.make_async_remote_copy(
            src_ref=src, dst_ref=dst, send_sem=send, recv_sem=recv,
            device_id=peer, device_id_type=MESH,
        )

    started = []

    def start(copies):
        for copy in copies:
            copy.start()
        started.extend(copies)

    def arrived(copies):
        for copy in copies:
            copy.wait_recv()

    ids_i = ids[...]
    ids_f = ids_i.astype(F32)
    rows = [ids_f[k : k + 1, :] for k in range(2)]
    ahead = lax.rem(lax.div(ids_i, G) - n + N, N)
    base = (lax.rem(ids_i, G) * N + ahead) * CAP
    base = jnp.where(ids_i < N * G, base, -CAP * T).astype(F32)
    cols = [jnp.broadcast_to(row, (T, T)).T for row in rows]
    earlier = lax.broadcasted_iota(jnp.int32, (T, T), 0) < lax.broadcasted_iota(jnp.int32, (T, T), 1)
    slot = lax.broadcasted_iota(jnp.int32, (N * A, T), 0).astype(F32)
    for k in range(2):
        same = jnp.where(cols[0] == rows[k], 1.0, 0.0) + jnp.where(cols[1] == rows[k], 1.0, 0.0)
        rank = jnp.sum(jnp.where(earlier, same, 0.0), axis=0, keepdims=True)
        target = base[k : k + 1, :] + rank
        place[:, k * T : (k + 1) * T] = jnp.where(slot == target, 1.0, 0.0).astype(BF)

    @functools.cache
    def y_copies(which):
        return [
            remote(
                ysend.at[which, lax.rem(g + j, G)], yrecv.at[which, :, g],
                y_send.at[which, j - 1], y_recv.at[which, j - 1], {"grp": lax.rem(g + j, G)},
            )
            for j in range(1, G)
        ]

    def lay(which):
        if which == 0:
            got = dot(place[:, 0:T] + place[:, T : 2 * T], tok[...], 1, 1)
        else:
            wide = cot[...].astype(F32)
            grads = [(gates[k : k + 1, :] * wide).astype(BF) for k in range(2)]
            got = dot(place[...], jnp.concatenate(grads, axis=1), 1, 1)
        got = got.reshape(G, 2, Q, F)
        for h in range(2):
            ysend[which, :, h] = got[:, h, :, 0:128].astype(BF)
            ysend[which, :, 2, :, h * FB : (h + 1) * FB] = got[:, h, :, 128:F].astype(BF)

    def shuffle(groups):
        size = 4 * groups * CAP
        i = lax.broadcasted_iota(jnp.int32, (size, size), 0)
        j = lax.broadcasted_iota(jnp.int32, (size, size), 1)
        e, v, c = i // (4 * CAP), lax.rem(i // CAP, 4), lax.rem(i, CAP)
        return jnp.where(j == (v * groups + e) * CAP + c, 1.0, 0.0).astype(BF)

    def y_to_z(source, target):
        for q in range(K):
            h, w = q // (K // 2), q % (K // 2)
            span = slice(w * 16, w * 16 + 16)
            a = source[h, :, span, :].reshape(4 * A, 128)
            target[4 * q : 4 * q + 4, 0:A, :] = dot(mix_a, a, 0, 0).astype(BF).reshape(4, A, 128)
            b = source[2, :, span, :].reshape(4 * A, 128)
            for c in range(2):
                part = dot(mix_b, b[c * 4 * B : (c + 1) * 4 * B], 0, 0)
                if c != h:
                    part = pltpu.roll(part, FB, 1)
                target[4 * q : 4 * q + 4, A : A + B, c * FB : (c + 1) * FB] = (
                    part[:, c * FB : (c + 1) * FB].astype(BF).reshape(4, B, FB)
                )

    def z_to_y(source, target):
        for q in range(K):
            h, w = q // (K // 2), q % (K // 2)
            span = slice(w * 16, w * 16 + 16)
            a = source[4 * q : 4 * q + 4, 0:A, :].reshape(4 * A, 128)
            target[:, h, span, :] = dot(mix_a, a, 1, 0).astype(BF).reshape(G, 16, 128)
            b = dot(mix_b, source[4 * q : 4 * q + 4, A : A + B, :].reshape(4 * B, 128), 1, 0)
            turned = pltpu.roll(b, FB, 1)
            for c in range(2):
                piece = (b if c == h else turned)[:, h * FB : (h + 1) * FB]
                target[c * C : (c + 1) * C, 2, span, h * FB : (h + 1) * FB] = (
                    piece.astype(BF).reshape(C, 16, FB)
                )

    near_first = [0]
    for j in range(1, M):
        near_first += [j, N - j]
    near_first.append(M)
    spot = {j: i for i, j in enumerate(near_first)}

    @functools.cache
    def z_copies(which, part):
        return [
            remote(
                zsend.at[which, N - j], zrecv.at[which, spot[j]],
                z_send.at[which, j - 1], z_recv.at[which, j - 1], {"node": lax.rem(n + N - j, N)},
            )
            for j in near_first[part * M : (part + 1) * M]
            if j
        ]

    @functools.cache
    def x_copies(which, part, stage):
        own = xall.at[which, part, r]
        top, low = own.at[pl.ds(0, HF)], own.at[pl.ds(HF, HF)]
        if stage == 0:
            pair = top, low
        elif stage == 1:
            pair = low, top
        else:
            pair = (
                xall.at[which, part, left_x, pl.ds(0, HF)],
                xall.at[which, part, right_x, pl.ds(HF, HF)],
            )
        return [
            remote(
                ref, ref, x_send.at[which, part, stage, i], x_recv.at[which, part, stage, i],
                {"rep": (right_x, left_x)[i]},
            )
            for i, ref in enumerate(pair)
        ]

    def unpack(which, part):
        arrived(z_copies(which, part))
        nodes = slice(part * M, (part + 1) * M)
        low = zrecv[which, nodes, A : A + B, :].reshape(W, 128).T
        for c in range(2):
            lanes = slice(c * W, (c + 1) * W)
            a = zrecv[which, nodes, c * B : (c + 1) * B, :].reshape(W, 128)
            xall[which, part, r, 0:128, lanes] = a.T
            xall[which, part, r, 128:F, lanes] = low[c * FB : (c + 1) * FB]
        start(x_copies(which, part, 0))
        start(x_copies(which, part, 1))

    def relay(which, part):
        for i in range(2):
            x_copies(which, part, 0)[i].wait_recv()
            start([x_copies(which, part, 2)[i]])

    def gathered(which, part):
        arrived(x_copies(which, part, 1))
        arrived(x_copies(which, part, 2))
        return xall[which, part].reshape(D, 2 * W)

    def widen(column, width):
        return jnp.concatenate([column] * (width // 128), axis=1) if width >= 128 else column[:, :width]

    @functools.cache
    def r_copies(way, part, stage):
        found = []
        for i in range(2):
            peer = {"rep": (left_x, right_x)[i]}
            if stage == 0:
                src, dst = xhalf.at[way, part, i], rhalf.at[way, part, i]
            else:
                span = pl.ds(HF if (i == 0) == (stage == 1) else 0, HF)
                src, dst = xfull.at[way, part, i, span], rfull.at[way, part, i, span]
            found.append(
                remote(src, dst, r_send.at[way, part, stage, i], r_recv.at[way, part, stage, i], peer)
            )
        return found

    def partial(way, part, target):
        span = pl.ds(pl.multiple_of(target * F, F), F)
        if way == 0:
            return dot(w_out_t[span, :], hid[part], 1, 0)
        return dot(w_in[span, :], d_pre[part], 1, 0)

    def sums_start(way, part):
        far = partial(way, part, far_x).astype(BF)
        xhalf[way, part, 0] = far[0:HF]
        xhalf[way, part, 1] = far[HF:F]
        start(r_copies(way, part, 0))
        for i, target in ((0, left_x), (1, right_x)):
            xfull[way, part, i] = partial(way, part, target).astype(BF)
            start([r_copies(way, part, 1)[i]])

    def sums_middle(way, part):
        for i in range(2):
            r_copies(way, part, 0)[i].wait_recv()
            span = slice(0, HF) if i == 0 else slice(HF, F)
            total = xfull[way, part, i, span].astype(F32) + rhalf[way, part, i].astype(F32)
            xfull[way, part, i, span] = total.astype(BF)
            start([r_copies(way, part, 2)[i]])

    @functools.cache
    def s_copies(way, part):
        return [
            remote(
                zback.at[way, spot[j]], zret.at[way, N - j],
                s_send.at[way, j - 1], s_recv.at[way, j - 1], {"node": lax.rem(n + j, N)},
            )
            for j in near_first[part * M : (part + 1) * M]
            if j
        ]

    def sums_end(way, part):
        total = partial(way, part, r)
        if way == 0:
            total = total + widen(out_bias, 2 * W)
        for i in range(2):
            r_copies(way, part, 1)[i].wait_recv()
            r_copies(way, part, 2)[i].wait_recv()
            total = total + rfull[way, part, i].astype(F32)
        value = total.astype(BF)
        nodes = slice(part * M, (part + 1) * M)
        low = jnp.concatenate([value[128:F, 0:W], value[128:F, W : 2 * W]], axis=0)
        zback[way, nodes, A : A + B, :] = low.T.reshape(M, B, 128)
        for c in range(2):
            zback[way, nodes, c * B : (c + 1) * B, :] = (
                value[0:128, c * W : (c + 1) * W].T.reshape(M, B, 128)
            )
        start(s_copies(way, part))
        if part == 0:
            zret[way, 0] = zback[way, 0]

    @functools.cache
    def b_copies(way):
        return [
            remote(
                back.at[way, lax.rem(g + j, G)], yret.at[way, :, g],
                b_send.at[way, j - 1], b_recv.at[way, j - 1], {"grp": lax.rem(g + j, G)},
            )
            for j in range(1, G)
        ]

    def homeward(way):
        for part in range(2):
            arrived(s_copies(way, part))
        z_to_y(zret.at[way], back.at[way])
        start(b_copies(way))
        yret[way, :, g] = back[way, g]

    def landed(way):
        arrived(b_copies(way))
        hot = place[...] if way == 0 else place[:, 0:T] + place[:, T : 2 * T]
        width = hot.shape[1]
        hot = hot.reshape(G, 2, Q, width)
        low = yret[way, 2].reshape(G * Q, 128)
        top, rest = 0.0, 0.0
        for h in range(2):
            one = hot[:, h].reshape(G * Q, width)
            top += dot(yret[way, h].reshape(G * Q, 128), one, 0, 0)
            rest += dot(low, one, 0, 0)[h * FB : (h + 1) * FB]
        return jnp.concatenate([top, rest], axis=0)

    def forward(part):
        x = gathered(0, part)
        acc = dot(w_in[...], x, 0, 0) + widen(bias, 2 * W)
        t = jnp.tanh(ROOT * (acc + 0.044715 * acc * acc * acc))
        hid[part] = (0.5 * acc * (1.0 + t)).astype(BF)
        dgelu[part] = 0.5 * (1.0 + t) + 0.5 * acc * (1.0 - t * t) * (
            ROOT * (1.0 + 3 * 0.044715 * acc * acc)
        )

    def backward(part):
        slope = dot(w_out[...], gathered(1, part), 1, 0)
        d_pre[part] = (slope * dgelu[part]).astype(BF)

    lay(0)
    pl.semaphore_wait(barrier, len(peers))
    start(y_copies(0))
    yrecv[0, :, g] = ysend[0, g]
    lay(1)
    start(y_copies(1))
    yrecv[1, :, g] = ysend[1, g]
    far, level = 1, 0
    while far < M:
        for j in (far, N - far):
            pl.semaphore_signal(
                reach.at[level], inc=1, device_id={"node": lax.rem(n + j, N)}, device_id_type=MESH
            )
        pl.semaphore_wait(reach.at[level], 2)
        far, level = 2 * far, level + 1
    mix_a, mix_b = shuffle(G), shuffle(C)
    for which in range(2):
        arrived(y_copies(which))
        y_to_z(yrecv.at[which], zsend.at[which])
        start(z_copies(which, 0))
        start(z_copies(which, 1))
        zrecv[which, 0] = zsend[which, 0]
    for copy in weights:
        copy.wait()
    w_out_t[...] = w_out[...].T
    bias = jnp.broadcast_to(b_in[...], (128, H)).T
    out_bias = jnp.broadcast_to(b_out[...], (128, F)).T

    unpack(0, 0)
    relay(0, 0)
    unpack(0, 1)
    relay(0, 1)
    forward(0)
    unpack(1, 0)
    sums_start(0, 0)
    forward(1)
    relay(1, 0)
    sums_middle(0, 0)
    sums_start(0, 1)
    unpack(1, 1)
    backward(0)
    sums_start(1, 0)
    relay(1, 1)
    sums_middle(0, 1)
    sums_end(0, 0)
    sums_middle(1, 0)
    backward(1)
    sums_start(1, 1)
    sums_end(0, 1)
    sums_end(1, 0)
    sums_middle(1, 1)

    ones = jnp.ones((8, 2 * W), BF)
    grad_in[...] = sum(dot(xall[0, part].reshape(D, 2 * W), d_pre[part], 1, 1) for part in range(2))
    outs = [
        pltpu.make_async_copy(grad_in, d_w_in, o_sem.at[0]),
        pltpu.make_async_copy(grad_out, d_w_out, o_sem.at[1]),
    ]
    outs[0].start()
    sums_end(1, 1)
    grad_out[...] = sum(dot(hid[part], xall[1, part].reshape(D, 2 * W), 1, 1) for part in range(2))
    outs[1].start()
    d_b_in[...] = sum(dot(ones, d_pre[part], 1, 1) for part in range(2))[0:1]
    d_b_out[...] = sum(dot(ones, xall[1, part, r], 1, 1) for part in range(2))[0:1]

    homeward(0)
    both = landed(0)
    wide = cot[...].astype(F32)
    cut = [both[:, k * T : (k + 1) * T] for k in range(2)]
    mixed[...] = (gates[0:1, :] * cut[0] + gates[1:2, :] * cut[1]).astype(BF)
    sums = [jnp.sum(one * wide, axis=0, keepdims=True) for one in cut]
    sums = jnp.concatenate(sums + [jnp.zeros((6, T), F32)], axis=0)
    dsum[...] = sums
    shares = [
        remote(dsum, drecv.at[j - 1], p_send.at[j - 1], p_recv.at[j - 1], {"rep": lax.rem(r + j, R)})
        for j in range(1, R)
    ]
    start(shares)
    homeward(1)
    arrived(shares)
    for j in range(R - 1):
        sums = sums + drecv[j]
    d_gates[...] = sums[0:2]
    d_tok[...] = landed(1).astype(BF)
    for copy in outs:
        copy.wait()
    for copy in started:
        copy.wait_send()


def hand_out(*refs):
    count = len(refs) // 3
    sources, results, held = refs[:count], refs[count : 2 * count], refs[2 * count : 3 * count]
    sem_in, sem_out = refs[3 * count :]
    inward = [pltpu.make_async_copy(s, h, sem_in.at[i]) for i, (s, h) in enumerate(zip(sources, held))]
    outward = [pltpu.make_async_copy(h, o, sem_out.at[i]) for i, (h, o) in enumerate(zip(held, results))]
    for copy in inward:
        copy.start()
    for i, copy in enumerate(inward):
        copy.wait()
        outward[i].start()
    for copy in outward:
        copy.wait()


def per_device(tokens, gates, expert_ids, w_in, b_in, w_out, b_out, cotangent):
    N, G, R = lax.axis_size("node"), lax.axis_size("grp"), lax.axis_size("rep")
    T, F = tokens.shape
    _, D, H = w_in.shape
    A, B, Q = G * CAP, G * CAP // 2, 2 * N
    W = N // 2 * B
    HF = F // 2
    dma = pltpu.SemaphoreType.DMA
    vmem = pl.BlockSpec(memory_space=pltpu.VMEM)
    any_ = pl.BlockSpec(memory_space=pl.ANY)
    shapes = (
        jax.ShapeDtypeStruct((F, T), BF),
        jax.ShapeDtypeStruct((F, T), BF),
        jax.ShapeDtypeStruct((2, T), F32),
        jax.ShapeDtypeStruct((D, H), F32),
        jax.ShapeDtypeStruct((1, H), F32),
        jax.ShapeDtypeStruct((H, D), F32),
        jax.ShapeDtypeStruct((1, F), F32),
    )
    out = pl.pallas_call(
        functools.partial(fused, N, G, R),
        out_shape=shapes,
        in_specs=[vmem, vmem, vmem, vmem, any_, vmem, any_, vmem],
        out_specs=(vmem, vmem, vmem, any_, vmem, any_, vmem),
        scratch_shapes=[
            pltpu.VMEM((N * A, 2 * T), BF),
            pltpu.VMEM((2, G, 3, Q, 128), BF),
            pltpu.VMEM((2, 3, G, Q, 128), BF),
            pltpu.VMEM((2, N, A + B, 128), BF),
            pltpu.VMEM((2, N, A + B, 128), BF),
            pltpu.VMEM((2, 2, R, F, 2 * W), BF),
            pltpu.VMEM((D, H), BF),
            pltpu.VMEM((H, D), BF),
            pltpu.VMEM((D, H), BF),
            pltpu.VMEM((2, H, 2 * W), F32),
            pltpu.VMEM((2, H, 2 * W), BF),
            pltpu.VMEM((2, H, 2 * W), BF),
            pltpu.VMEM((2, 2, 2, HF, 2 * W), BF),
            pltpu.VMEM((2, 2, 2, F, 2 * W), BF),
            pltpu.VMEM((2, 2, 2, HF, 2 * W), BF),
            pltpu.VMEM((2, 2, 2, F, 2 * W), BF),
            pltpu.VMEM((2, N, A + B, 128), BF),
            pltpu.VMEM((2, N, A + B, 128), BF),
            pltpu.VMEM((2, G, 3, Q, 128), BF),
            pltpu.VMEM((2, 3, G, Q, 128), BF),
            pltpu.VMEM((D, H), F32),
            pltpu.VMEM((H, D), F32),
            pltpu.VMEM((8, T), F32),
            pltpu.VMEM((R - 1, 8, T), F32),
            dma((2, G - 1)),
            dma((2, G - 1)),
            dma((2, N - 1)),
            dma((2, N - 1)),
            dma((2, 2, 3, 2)),
            dma((2, 2, 3, 2)),
            dma((2, 2, 3, 2)),
            dma((2, 2, 3, 2)),
            dma((2, N - 1)),
            dma((2, N - 1)),
            dma((2, G - 1)),
            dma((2, G - 1)),
            dma((R - 1,)),
            dma((R - 1,)),
            dma((4,)),
            pltpu.SemaphoreType.REGULAR((4,)),
        ],
        compiler_params=pltpu.CompilerParams(
            collective_id=0, has_side_effects=True, vmem_limit_bytes=60 * 2**20
        ),
    )(
        tokens.T, cotangent.T, expert_ids.T, gates.T,
        w_in[0], b_in, w_out[0], b_out,
    )
    out = pl.pallas_call(
        hand_out,
        out_shape=shapes,
        in_specs=[any_] * 7,
        out_specs=(any_,) * 7,
        scratch_shapes=[pltpu.VMEM(one.shape, one.dtype) for one in shapes] + [dma((7,)), dma((7,))],
    )(*out)
    mixed, d_tok, d_gates, d_w_in, d_b_in, d_w_out, d_b_out = out
    return (mixed.T, d_tok.T, d_gates.T, d_w_in[None], d_b_in, d_w_out[None], d_b_out)


def solution(mesh):
    both = ("node", "grp")
    return jax.shard_map(
        per_device,
        mesh=mesh,
        in_specs=(
            P(both, "rep"),
            P(both, None),
            P(both, None),
            P(both, None, "rep"),
            P(both, "rep"),
            P(both, "rep", None),
            P(both, "rep"),
            P(both, "rep"),
        ),
        out_specs=(
            P(both, "rep"),
            P(both, "rep"),
            P(both, None),
            P(both, None, "rep"),
            P(both, "rep"),
            P(both, "rep", None),
            P(both, "rep"),
        ),
        check_vma=False,
    )
```

time: 95.8 us -> 87.1 us (0.909)
  Pallas kernels: 94.9 us -> 86.2 us
    pallas_call x1, Pallas kernels: 92.1 us -> 83.4 us  [per_device(): pl.pallas_call(functools.partial(fused, N, G, R), out_shape=shapes, in_sp...]
where the time goes in v3:
time: 87.1 us; the launch traced here: 86.9 us
  Pallas kernels  86.2 us (99%)
    pallas_call x1, Pallas kernels, per_device(): pl.pallas_call(functools.partial(fused, N, G, R), out_shape=shapes, in_sp...  83.4 us
    pallas_call x1, Pallas kernels, per_device(): pl.pallas_call(hand_out, out_shape=shapes, in_specs=[any_] * 7, out_specs...  2.86 us

profile of v3, /device:TPU:1, one launch (start us, length us, event | category | flops | bytes accessed | tf_op | source)
XLA Modules:
  0.0 86.9 jit_solution(13473763516920617650)
XLA Ops:
  0.6 83.4 %shard_map.135 = (bf16[192,128]{1,0:T(8,128)(2,1)}, bf16[192,128]{1,0:T(8,128)(2,1)}, f32[2,128]{1,0:T(2,128)}, f32[768,384]{1,0:T(8,128)}, f32[1,384]{1,0:T(1,1...) custom-call(bf16[192,128]{1,0:T(8,128)(2,1)} %bitcast.13, bf16[192,128]{1,0:T(8,128)(2,1)} %bitcast.14, s32[2,128]{1,0:T(2,128)} %bitcast.15, ...), custom_call_target="tpu_custom_call" | custom-call | tf_op jit(solution)/shard_map/pallas_call | solution.py:449
  84.0 2.9 %shard_map.136 = (bf16[192,128]{1,0:T(8,128)(2,1)}, bf16[192,128]{1,0:T(8,128)(2,1)}, f32[2,128]{1,0:T(2,128)}, f32[768,384]{1,0:T(8,128)}, f32[1,384]{1,0:T(1,1...) custom-call(bf16[192,128]{1,0:T(8,128)(2,1)} %get-tuple-element.21.refs_0_, bf16[192,128]{1,0:T(8,128)(2,1)} %get-tuple-element.22.refs_1_, ...), custom_call_target="tpu_custom_call" | custom-call | tf_op jit(solution)/shard_map/pallas_call | solution.py:503

commit v4 on v3

--- a/solution.py
+++ b/solution.py
@@ -10,6 +10,7 @@
 
 MESH = pl.DeviceIdType.MESH
 CAP = 4
+VLIM = 60
 BF = jnp.bfloat16
 F32 = jnp.float32
 ROOT = math.sqrt(2.0 / math.pi)
@@ -77,7 +78,13 @@
     ids_i = ids[...]
     ids_f = ids_i.astype(F32)
     rows = [ids_f[k : k + 1, :] for k in range(2)]
-    ahead = lax.rem(lax.div(ids_i, G) - n + N, N)
+    near_first = [0]
+    for j in range(1, M):
+        near_first += [j, N - j]
+    near_first.append(M)
+    spot = {j: i for i, j in enumerate(near_first)}
+    away = lax.rem(n + 16 * N - lax.div(ids_i, G), N)
+    ahead = sum(jnp.where(away == j, spot[j], 0) for j in range(1, N))
     base = (lax.rem(ids_i, G) * N + ahead) * CAP
     base = jnp.where(ids_i < N * G, base, -CAP * T).astype(F32)
     cols = [jnp.broadcast_to(row, (T, T)).T for row in rows]
@@ -90,11 +97,11 @@
         place[:, k * T : (k + 1) * T] = jnp.where(slot == target, 1.0, 0.0).astype(BF)
 
     @functools.cache
-    def y_copies(which):
+    def y_copies(which, part):
         return [
             remote(
-                ysend.at[which, lax.rem(g + j, G)], yrecv.at[which, :, g],
-                y_send.at[which, j - 1], y_recv.at[which, j - 1], {"grp": lax.rem(g + j, G)},
+                ysend.at[which, part, lax.rem(g + j, G)], yrecv.at[which, part, g],
+                y_send.at[which, part, j - 1], y_recv.at[which, part, j - 1], {"grp": lax.rem(g + j, G)},
             )
             for j in range(1, G)
         ]
@@ -108,8 +115,15 @@
             got = dot(place[...], jnp.concatenate(grads, axis=1), 1, 1)
         got = got.reshape(G, 2, Q, F)
         for h in range(2):
-            ysend[which, :, h] = got[:, h, :, 0:128].astype(BF)
-            ysend[which, :, 2, :, h * FB : (h + 1) * FB] = got[:, h, :, 128:F].astype(BF)
+            ysend[which, h, :, 0:Q] = got[:, h, :, 0:128].astype(BF)
+            for w in range(K // 2):
+                ysend[which, h, :, Q : Q + 16, w * FB : (w + 1) * FB] = (
+                    got[:, h, w * 16 : (w + 1) * 16, 128:F].astype(BF)
+                )
+
+    def y_start(which, part):
+        start(y_copies(which, part))
+        yrecv[which, part, g] = ysend[which, part, g]
 
     def shuffle(groups):
         size = 4 * groups * CAP
@@ -118,49 +132,46 @@
         e, v, c = i // (4 * CAP), lax.rem(i // CAP, 4), lax.rem(i, CAP)
         return jnp.where(j == (v * groups + e) * CAP + c, 1.0, 0.0).astype(BF)
 
-    def y_to_z(source, target):
-        for q in range(K):
-            h, w = q // (K // 2), q % (K // 2)
-            span = slice(w * 16, w * 16 + 16)
-            a = source[h, :, span, :].reshape(4 * A, 128)
+    def y_to_z(which, part):
+        arrived(y_copies(which, part))
+        source, target = yrecv.at[which, part], zsend.at[which]
+        b = source[:, Q : Q + 16, :].reshape(4 * A, 128)
+        for w in range(K // 2):
+            q = part * (K // 2) + w
+            a = source[:, w * 16 : w * 16 + 16, :].reshape(4 * A, 128)
             target[4 * q : 4 * q + 4, 0:A, :] = dot(mix_a, a, 0, 0).astype(BF).reshape(4, A, 128)
-            b = source[2, :, span, :].reshape(4 * A, 128)
             for c in range(2):
-                part = dot(mix_b, b[c * 4 * B : (c + 1) * 4 * B], 0, 0)
-                if c != h:
-                    part = pltpu.roll(part, FB, 1)
+                piece = dot(mix_b, b[c * 4 * B : (c + 1) * 4 * B], 0, 0)
+                if c != w:
+                    piece = pltpu.roll(piece, FB, 1)
                 target[4 * q : 4 * q + 4, A : A + B, c * FB : (c + 1) * FB] = (
-                    part[:, c * FB : (c + 1) * FB].astype(BF).reshape(4, B, FB)
+                    piece[:, c * FB : (c + 1) * FB].astype(BF).reshape(4, B, FB)
                 )
-
-    def z_to_y(source, target):
-        for q in range(K):
-            h, w = q // (K // 2), q % (K // 2)
-            span = slice(w * 16, w * 16 + 16)
+        start(z_copies(which, part))
+        if part == 0:
+            zrecv[which, 0] = zsend[which, 0]
+
+    def z_to_y(source, target, part):
+        for w in range(K // 2):
+            q = part * (K // 2) + w
             a = source[4 * q : 4 * q + 4, 0:A, :].reshape(4 * A, 128)
-            target[:, h, span, :] = dot(mix_a, a, 1, 0).astype(BF).reshape(G, 16, 128)
+            target[:, w * 16 : w * 16 + 16, :] = dot(mix_a, a, 1, 0).astype(BF).reshape(G, 16, 128)
             b = dot(mix_b, source[4 * q : 4 * q + 4, A : A + B, :].reshape(4 * B, 128), 1, 0)
             turned = pltpu.roll(b, FB, 1)
             for c in range(2):
-                piece = (b if c == h else turned)[:, h * FB : (h + 1) * FB]
-                target[c * C : (c + 1) * C, 2, span, h * FB : (h + 1) * FB] = (
+                piece = (b if c == w else turned)[:, w * FB : (w + 1) * FB]
+                target[c * C : (c + 1) * C, Q : Q + 16, w * FB : (w + 1) * FB] = (
                     piece.astype(BF).reshape(C, 16, FB)
                 )
-
-    near_first = [0]
-    for j in range(1, M):
-        near_first += [j, N - j]
-    near_first.append(M)
-    spot = {j: i for i, j in enumerate(near_first)}
 
     @functools.cache
     def z_copies(which, part):
         return [
             remote(
-                zsend.at[which, N - j], zrecv.at[which, spot[j]],
+                zsend.at[which, spot[j]], zrecv.at[which, spot[j]],
                 z_send.at[which, j - 1], z_recv.at[which, j - 1], {"node": lax.rem(n + N - j, N)},
             )
-            for j in near_first[part * M : (part + 1) * M]
+            for j in reversed(near_first[part * M : (part + 1) * M])
             if j
         ]
 
@@ -252,10 +263,10 @@
     def s_copies(way, part):
         return [
             remote(
-                zback.at[way, spot[j]], zret.at[way, N - j],
+                zback.at[way, spot[j]], zret.at[way, spot[j]],
                 s_send.at[way, j - 1], s_recv.at[way, j - 1], {"node": lax.rem(n + j, N)},
             )
-            for j in near_first[part * M : (part + 1) * M]
+            for j in reversed(near_first[part * M : (part + 1) * M])
             if j
         ]
 
@@ -280,33 +291,33 @@
             zret[way, 0] = zback[way, 0]
 
     @functools.cache
-    def b_copies(way):
+    def b_copies(way, part):
         return [
             remote(
-                back.at[way, lax.rem(g + j, G)], yret.at[way, :, g],
-                b_send.at[way, j - 1], b_recv.at[way, j - 1], {"grp": lax.rem(g + j, G)},
+                back.at[way, part, lax.rem(g + j, G)], yret.at[way, part, g],
+                b_send.at[way, part, j - 1], b_recv.at[way, part, j - 1], {"grp": lax.rem(g + j, G)},
             )
             for j in range(1, G)
         ]
 
-    def homeward(way):
-        for part in range(2):
-            arrived(s_copies(way, part))
-        z_to_y(zret.at[way], back.at[way])
-        start(b_copies(way))
-        yret[way, :, g] = back[way, g]
+    def homeward(way, part):
+        arrived(s_copies(way, part))
+        z_to_y(zret.at[way], back.at[way, part], part)
+        start(b_copies(way, part))
+        yret[way, part, g] = back[way, part, g]
 
     def landed(way):
-        arrived(b_copies(way))
         hot = place[...] if way == 0 else place[:, 0:T] + place[:, T : 2 * T]
         width = hot.shape[1]
         hot = hot.reshape(G, 2, Q, width)
-        low = yret[way, 2].reshape(G * Q, 128)
         top, rest = 0.0, 0.0
-        for h in range(2):
-            one = hot[:, h].reshape(G * Q, width)
-            top += dot(yret[way, h].reshape(G * Q, 128), one, 0, 0)
-            rest += dot(low, one, 0, 0)[h * FB : (h + 1) * FB]
+        for h in (0, 1):
+            arrived(b_copies(way, h))
+            top += dot(yret[way, h, :, 0:Q].reshape(G * Q, 128), hot[:, h].reshape(G * Q, width), 0, 0)
+            low = yret[way, h, :, Q : Q + 16].reshape(G * 16, 128)
+            for w in range(K // 2):
+                one = hot[:, h, w * 16 : (w + 1) * 16].reshape(G * 16, width)
+                rest += dot(low, one, 0, 0)[w * FB : (w + 1) * FB]
         return jnp.concatenate([top, rest], axis=0)
 
     def forward(part):
@@ -322,28 +333,37 @@
         slope = dot(w_out[...], gathered(1, part), 1, 0)
         d_pre[part] = (slope * dgelu[part]).astype(BF)
 
-    lay(0)
-    pl.semaphore_wait(barrier, len(peers))
-    start(y_copies(0))
-    yrecv[0, :, g] = ysend[0, g]
-    lay(1)
-    start(y_copies(1))
-    yrecv[1, :, g] = ysend[1, g]
-    far, level = 1, 0
-    while far < M:
-        for j in (far, N - far):
+    rounds = []
+    while 2 ** len(rounds) < M:
+        rounds.append(2 ** len(rounds))
+
+    def tell(level):
+        for j in (rounds[level], N - rounds[level]):
             pl.semaphore_signal(
                 reach.at[level], inc=1, device_id={"node": lax.rem(n + j, N)}, device_id_type=MESH
             )
+
+    def hear(level):
         pl.semaphore_wait(reach.at[level], 2)
-        far, level = 2 * far, level + 1
+
+    last = len(rounds) - 1
     mix_a, mix_b = shuffle(G), shuffle(C)
-    for which in range(2):
-        arrived(y_copies(which))
-        y_to_z(yrecv.at[which], zsend.at[which])
-        start(z_copies(which, 0))
-        start(z_copies(which, 1))
-        zrecv[which, 0] = zsend[which, 0]
+    lay(0)
+    lay(1)
+    pl.semaphore_wait(barrier, len(peers))
+    tell(0)
+    y_start(0, 0)
+    y_start(0, 1)
+    for level in range(last):
+        hear(level)
+        tell(level + 1)
+    y_start(1, 0)
+    y_start(1, 1)
+    y_to_z(0, 0)
+    hear(last)
+    y_to_z(0, 1)
+    y_to_z(1, 0)
+    y_to_z(1, 1)
     for copy in weights:
         copy.wait()
     w_out_t[...] = w_out[...].T
@@ -387,7 +407,9 @@
     d_b_in[...] = sum(dot(ones, d_pre[part], 1, 1) for part in range(2))[0:1]
     d_b_out[...] = sum(dot(ones, xall[1, part, r], 1, 1) for part in range(2))[0:1]
 
-    homeward(0)
+    homeward(0, 0)
+    homeward(0, 1)
+    homeward(1, 0)
     both = landed(0)
     wide = cot[...].astype(F32)
     cut = [both[:, k * T : (k + 1) * T] for k in range(2)]
@@ -400,7 +422,7 @@
         for j in range(1, R)
     ]
     start(shares)
-    homeward(1)
+    homeward(1, 1)
     arrived(shares)
     for j in range(R - 1):
         sums = sums + drecv[j]
@@ -416,13 +438,20 @@
     count = len(refs) // 3
     sources, results, held = refs[:count], refs[count : 2 * count], refs[2 * count : 3 * count]
     sem_in, sem_out = refs[3 * count :]
-    inward = [pltpu.make_async_copy(s, h, sem_in.at[i]) for i, (s, h) in enumerate(zip(sources, held))]
-    outward = [pltpu.make_async_copy(h, o, sem_out.at[i]) for i, (h, o) in enumerate(zip(held, results))]
+    parts = []
+    for source, result, kept in zip(sources, results, held):
+        size = source.shape[0]
+        step = size // 4 if size >= 256 else size
+        for i in range(0, size, step):
+            span = pl.ds(i, step)
+            parts.append((source.at[span], kept.at[span], result.at[span]))
+    inward = [pltpu.make_async_copy(a, b, sem_in.at[i]) for i, (a, b, _) in enumerate(parts)]
+    outward = [pltpu.make_async_copy(b, c, sem_out.at[i]) for i, (_, b, c) in enumerate(parts)]
     for copy in inward:
         copy.start()
-    for i, copy in enumerate(inward):
+    for copy, onward in zip(inward, outward):
         copy.wait()
-        outward[i].start()
+        onward.start()
     for copy in outward:
         copy.wait()
 
@@ -453,8 +482,8 @@
         out_specs=(vmem, vmem, vmem, any_, vmem, any_, vmem),
         scratch_shapes=[
             pltpu.VMEM((N * A, 2 * T), BF),
-            pltpu.VMEM((2, G, 3, Q, 128), BF),
-            pltpu.VMEM((2, 3, G, Q, 128), BF),
+            pltpu.VMEM((2, 2, G, Q + 16, 128), BF),
+            pltpu.VMEM((2, 2, G, Q + 16, 128), BF),
             pltpu.VMEM((2, N, A + B, 128), BF),
             pltpu.VMEM((2, N, A + B, 128), BF),
             pltpu.VMEM((2, 2, R, F, 2 * W), BF),
@@ -470,14 +499,14 @@
             pltpu.VMEM((2, 2, 2, F, 2 * W), BF),
             pltpu.VMEM((2, N, A + B, 128), BF),
             pltpu.VMEM((2, N, A + B, 128), BF),
-            pltpu.VMEM((2, G, 3, Q, 128), BF),
-            pltpu.VMEM((2, 3, G, Q, 128), BF),
+            pltpu.VMEM((2, 2, G, Q + 16, 128), BF),
+            pltpu.VMEM((2, 2, G, Q + 16, 128), BF),
             pltpu.VMEM((D, H), F32),
             pltpu.VMEM((H, D), F32),
             pltpu.VMEM((8, T), F32),
             pltpu.VMEM((R - 1, 8, T), F32),
-            dma((2, G - 1)),
-            dma((2, G - 1)),
+            dma((2, 2, G - 1)),
+            dma((2, 2, G - 1)),
             dma((2, N - 1)),
             dma((2, N - 1)),
             dma((2, 2, 3, 2)),
@@ -486,15 +515,15 @@
             dma((2, 2, 3, 2)),
             dma((2, N - 1)),
             dma((2, N - 1)),
-            dma((2, G - 1)),
-            dma((2, G - 1)),
+            dma((2, 2, G - 1)),
+            dma((2, 2, G - 1)),
             dma((R - 1,)),
             dma((R - 1,)),
             dma((4,)),
             pltpu.SemaphoreType.REGULAR((4,)),
         ],
         compiler_params=pltpu.CompilerParams(
-            collective_id=0, has_side_effects=True, vmem_limit_bytes=60 * 2**20
+            collective_id=0, has_side_effects=True, vmem_limit_bytes=VLIM * 2**20
         ),
     )(
         tokens.T, cotangent.T, expert_ids.T, gates.T,
@@ -505,7 +534,7 @@
         out_shape=shapes,
         in_specs=[any_] * 7,
         out_specs=(any_,) * 7,
-        scratch_shapes=[pltpu.VMEM(one.shape, one.dtype) for one in shapes] + [dma((7,)), dma((7,))],
+        scratch_shapes=[pltpu.VMEM(one.shape, one.dtype) for one in shapes] + [dma((13,)), dma((13,))],
     )(*out)
     mixed, d_tok, d_gates, d_w_in, d_b_in, d_w_out, d_b_out = out
     return (mixed.T, d_tok.T, d_gates.T, d_w_in[None], d_b_in, d_w_out[None], d_b_out)

time: 87.1 us -> 82 us (0.941)
  Pallas kernels: 86.2 us -> 81.1 us
    pallas_call x1, Pallas kernels: 83.4 us -> 78.5 us  [per_device(): pl.pallas_call(functools.partial(fused, N, G, R), out_shape=shapes, in_sp...]
where the time goes in v4:
time: 82 us; the launch traced here: 81.8 us
  Pallas kernels  81.1 us (99%)
    pallas_call x1, Pallas kernels, per_device(): pl.pallas_call(functools.partial(fused, N, G, R), out_shape=shapes, in_sp...  78.5 us
    pallas_call x1, Pallas kernels, per_device(): pl.pallas_call(hand_out, out_shape=shapes, in_specs=[any_] * 7, out_specs...  2.65 us

profile of v4, /device:TPU:1, one launch (start us, length us, event | category | flops | bytes accessed | tf_op | source)
XLA Modules:
  0.0 81.8 jit_solution(6162268552951511242)
XLA Ops:
  0.6 78.5 %shard_map.135 = (bf16[192,128]{1,0:T(8,128)(2,1)}, bf16[192,128]{1,0:T(8,128)(2,1)}, f32[2,128]{1,0:T(2,128)}, f32[768,384]{1,0:T(8,128)}, f32[1,384]{1,0:T(1,1...) custom-call(bf16[192,128]{1,0:T(8,128)(2,1)} %bitcast.13, bf16[192,128]{1,0:T(8,128)(2,1)} %bitcast.14, s32[2,128]{1,0:T(2,128)} %bitcast.15, ...), custom_call_target="tpu_custom_call" | custom-call | tf_op jit(solution)/shard_map/pallas_call | solution.py:478
  79.1 2.7 %shard_map.136 = (bf16[192,128]{1,0:T(8,128)(2,1)}, bf16[192,128]{1,0:T(8,128)(2,1)}, f32[2,128]{1,0:T(2,128)}, f32[768,384]{1,0:T(8,128)}, f32[1,384]{1,0:T(1,1...) custom-call(bf16[192,128]{1,0:T(8,128)(2,1)} %get-tuple-element.21.refs_0_, bf16[192,128]{1,0:T(8,128)(2,1)} %get-tuple-element.22.refs_1_, ...), custom_call_target="tpu_custom_call" | custom-call | tf_op jit(solution)/shard_map/pallas_call | solution.py:532

commit v5 on v4

--- a/solution.py
+++ b/solution.py
@@ -103,7 +103,7 @@
                 ysend.at[which, part, lax.rem(g + j, G)], yrecv.at[which, part, g],
                 y_send.at[which, part, j - 1], y_recv.at[which, part, j - 1], {"grp": lax.rem(g + j, G)},
             )
-            for j in range(1, G)
+            for j in sorted(range(1, G), key=lambda j: abs(j - G // 2))
         ]
 
     def lay(which):
@@ -297,7 +297,7 @@
                 back.at[way, part, lax.rem(g + j, G)], yret.at[way, part, g],
                 b_send.at[way, part, j - 1], b_recv.at[way, part, j - 1], {"grp": lax.rem(g + j, G)},
             )
-            for j in range(1, G)
+            for j in sorted(range(1, G), key=lambda j: abs(j - G // 2))
         ]
 
     def homeward(way, part):

time: 82 us -> 81.8 us (level)
  no operation moved by 1% of the time
where the time goes in v5:
time: 81.8 us; the launch traced here: 81.6 us
  Pallas kernels  81 us (99%)
    pallas_call x1, Pallas kernels, per_device(): pl.pallas_call(functools.partial(fused, N, G, R), out_shape=shapes, in_sp...  78.3 us
    pallas_call x1, Pallas kernels, per_device(): pl.pallas_call(hand_out, out_shape=shapes, in_specs=[any_] * 7, out_specs...  2.65 us

profile of v5, /device:TPU:1, one launch (start us, length us, event | category | flops | bytes accessed | tf_op | source)
XLA Modules:
  0.0 81.6 jit_solution(18156833625813251145)
XLA Ops:
  0.6 78.3 %shard_map.135 = (bf16[192,128]{1,0:T(8,128)(2,1)}, bf16[192,128]{1,0:T(8,128)(2,1)}, f32[2,128]{1,0:T(2,128)}, f32[768,384]{1,0:T(8,128)}, f32[1,384]{1,0:T(1,1...) custom-call(bf16[192,128]{1,0:T(8,128)(2,1)} %bitcast.13, bf16[192,128]{1,0:T(8,128)(2,1)} %bitcast.14, s32[2,128]{1,0:T(2,128)} %bitcast.15, ...), custom_call_target="tpu_custom_call" | custom-call | tf_op jit(solution)/shard_map/pallas_call | solution.py:478
  79.0 2.7 %shard_map.136 = (bf16[192,128]{1,0:T(8,128)(2,1)}, bf16[192,128]{1,0:T(8,128)(2,1)}, f32[2,128]{1,0:T(2,128)}, f32[768,384]{1,0:T(8,128)}, f32[1,384]{1,0:T(1,1...) custom-call(bf16[192,128]{1,0:T(8,128)(2,1)} %get-tuple-element.21.refs_0_, bf16[192,128]{1,0:T(8,128)(2,1)} %get-tuple-element.22.refs_1_, ...), custom_call_target="tpu_custom_call" | custom-call | tf_op jit(solution)/shard_map/pallas_call | solution.py:532
